TPU v7x, 128 devices: a whole 4x4x4 slice. The times are simulated.
128 devices in a mesh: lat: 8 (over x, y_lo), lon: 16 (over y_hi, z, core).
Axes of the slice: x: 4, y: 4 (y_hi: 2, y_lo: 2; y = y_hi * 2 + y_lo), z: 4, core: 2. Of those that a mesh axis runs over, the one named last changes fastest.
Arguments:
- innovations: float32 [25, 65536], P(None, ('lat', 'lon')), may hold values from -6 to 6
- owners: int32 [65536, 1], P(('lat', 'lon')), may hold values from 0 to 127, as said below
- prof_row: int32 [65536], P(('lat', 'lon')), may hold values from 0 to 254
- prof_col: int32 [65536], P(('lat', 'lon')), may hold values from 0 to 126
- interp_weights: float32 [4, 65536], P(None, ('lat', 'lon')), may hold values from 0.1 to 1
- model_tiles: float32 [25, 4096, 8, 128], P(None, ('lat', 'lon')), may hold values from -6 to 6
- model_ids: int32 [1, 4096], P(None, ('lat', 'lon')), may hold values from 0 to 31, as said below
- face_x: float32 [2048, 2048], P('lat', 'lon'), may hold values from 0.02 to 0.12
- face_y: float32 [2048, 2048], P('lat', 'lon'), may hold values from 0.02 to 0.12
- cross_term: float32 [2048, 2048], P('lat', 'lon'), may hold values from -0.08 to 0.08
- wet_mask: int32 [2048, 2048], P('lat', 'lon'), may hold values 0 or 1
- norm_factor: float32 [25, 2048, 2048], P(None, 'lat', 'lon'), may hold values from 0.4 to 2.5
Outputs:
- smoothed: float32 [25, 2048, 2048], P(None, 'lat', 'lon')
- profile_values: float32 [25, 65536], P(None, ('lat', 'lon'))
Inputs may be any that keep to these rules, and one draw needn't show every extreme that they name: `owners`: among the 512 profiles of one device no owner appears more than 8 times; in every draw one owner appears exactly 8 times among every device's profiles. Owners count analysis blocks in lat-major order. `model_ids`: the 32 slots of the model device at lat index i and lon index g form as many equal groups as the lon axis has devices; group j holds tiles of the analysis block at lat index i and lon index j, and every analysis block's 32 tiles appear exactly once over its lat row.
All inputs are finite; a program needn't handle non-finite values. No bound on the sum of `wet_mask` on one device may be relied on, other than what follows from the above.
Results may differ from a plain program's by a relative error of at most 0.00002.
Values sent between devices are 32-bit elements; how exact they have to be, the bound alone decides.
A program may use at most 128 MiB of HBM per device.

v0:
```python
import jax
import jax.numpy as jnp
from jax import lax
from jax.sharding import PartitionSpec as P

STEPS = 10


def with_halo(cells, sides, width, closed):
    for axis, dim in sides:
        count = lax.axis_size(axis)
        ends = count if closed else count - 1
        head = lax.slice_in_dim(cells, 0, width, axis=dim)
        tail = lax.slice_in_dim(cells, cells.shape[dim] - width, cells.shape[dim], axis=dim)
        cells = jnp.concatenate(
            [
                lax.ppermute(tail, axis, [(i, (i + 1) % count) for i in range(ends)]),
                cells,
                lax.ppermute(head, axis, [((i + 1) % count, i) for i in range(ends)]),
            ],
            axis=dim,
        )
    return cells


def rims(values, width):
    widened = with_halo(values, (("lon", 2),), width, True)
    return with_halo(widened, (("lat", 1),), width, False)


def face_weights(stack):
    face_east = stack[0]
    face_north = stack[1]
    twist_field = stack[2]
    wet_cells = stack[3]
    east_face = face_east[1:-1, 1:-1] * wet_cells[1:-1, 1:-1] * wet_cells[1:-1, 2:]
    west_face = face_east[1:-1, :-2] * wet_cells[1:-1, :-2] * wet_cells[1:-1, 1:-1]
    north_face = face_north[1:-1, 1:-1] * wet_cells[1:-1, 1:-1] * wet_cells[2:, 1:-1]
    south_face = face_north[:-2, 1:-1] * wet_cells[:-2, 1:-1] * wet_cells[1:-1, 1:-1]
    twist_face = twist_field[1:-1, 1:-1] * wet_cells[1:-1, 1:-1]
    return (east_face, west_face, north_face, south_face, twist_face)


def trimmed(weights, offset):
    height = weights[0].shape[0]
    across = weights[0].shape[1]
    return tuple(
        (weight[offset : height - offset, offset : across - offset][None] for weight in weights)
    )


def advance(padded, sectioned):
    east_face, west_face, north_face, south_face, twist_face = sectioned
    centre = padded[:, 1:-1, 1:-1]
    return (
        centre
        + east_face * (padded[:, 1:-1, 2:] - centre)
        + west_face * (padded[:, 1:-1, :-2] - centre)
        + north_face * (padded[:, 2:, 1:-1] - centre)
        + south_face * (padded[:, :-2, 1:-1] - centre)
        + 0.25
        * twist_face
        * (padded[:, 2:, 2:] - padded[:, 2:, :-2] - padded[:, :-2, 2:] + padded[:, :-2, :-2])
    )


def on_device(
    innovations,
    owners,
    prof_row,
    prof_col,
    interp_weights,
    model_tiles,
    model_ids,
    face_x,
    face_y,
    cross_term,
    wet_mask,
    norm_factor,
):
    levels = norm_factor.shape[0]
    lat_cells = norm_factor.shape[1]
    lon_cells = norm_factor.shape[2]
    moved_tiles, moved_ids = (
        lax.all_to_all(model_tiles, "lon", split_axis=1, concat_axis=1, tiled=True),
        lax.all_to_all(model_ids, "lon", split_axis=1, concat_axis=1, tiled=True),
    )
    increment = jnp.zeros_like(moved_tiles).at[:, moved_ids[0]].set(moved_tiles)
    increment = increment.reshape(levels, lat_cells, lon_cells)
    devices = lax.axis_size(("lat", "lon"))
    local_count = innovations.shape[1]
    capacity = 2 * local_count // devices
    owner_list = owners[:, 0]
    one_hot = (owner_list[:, None] == jnp.arange(devices, dtype=jnp.int32)[None, :]).astype(
        jnp.int32
    )
    running = jnp.cumsum(one_hot, axis=0)
    rank_in = jnp.sum(running * one_hot, axis=1) - 1
    slot_of = owner_list * capacity + rank_in
    payload = jnp.concatenate([innovations, interp_weights], axis=0)
    send_float = (
        jnp.zeros((levels + 4, devices * capacity), jnp.float32).at[:, slot_of].set(payload)
    )
    location = prof_row * lon_cells + prof_col
    send_index = jnp.zeros((1, devices * capacity), jnp.int32).at[0, slot_of].set(location)
    recv_float, recv_index = (
        lax.all_to_all(send_float, ("lat", "lon"), split_axis=1, concat_axis=1, tiled=True),
        lax.all_to_all(send_index, ("lat", "lon"), split_axis=1, concat_axis=1, tiled=True),
    )
    base_cell = recv_index[0]
    recv_values = recv_float[:levels]
    recv_weights = recv_float[levels:]
    corner_cells = jnp.concatenate(
        [base_cell, base_cell + 1, base_cell + lon_cells, base_cell + lon_cells + 1]
    )
    spread = jnp.concatenate(
        [recv_values * recv_weights[corner][None, :] for corner in range(4)], axis=1
    )
    observed = (
        jnp.zeros((levels, lat_cells * lon_cells), jnp.float32).at[:, corner_cells].add(spread)
    )
    observed = observed.reshape(levels, lat_cells, lon_cells)
    field = norm_factor * (observed + increment)
    depth = 1
    stacked = jnp.stack([face_x, face_y, cross_term, wet_mask.astype(jnp.float32)])
    weights = face_weights(rims(stacked, depth + 1))
    sectioned_list = [trimmed(weights, 1)]

    def sweep(number, values):
        padded = rims(values, depth)
        padded = advance(padded, sectioned_list[0])
        return padded

    field = lax.fori_loop(0, STEPS // depth, sweep, field)
    smoothed = norm_factor * field
    flat_field = smoothed.reshape(levels, -1)
    sampled = (
        recv_weights[0][None, :] * flat_field[:, base_cell]
        + recv_weights[1][None, :] * flat_field[:, base_cell + 1]
        + recv_weights[2][None, :] * flat_field[:, base_cell + lon_cells]
        + recv_weights[3][None, :] * flat_field[:, base_cell + lon_cells + 1]
    )
    returned = lax.all_to_all(sampled, ("lat", "lon"), split_axis=1, concat_axis=1, tiled=True)
    profile_values = returned[:, slot_of]
    return (smoothed, profile_values)


def solution(mesh):
    in_specs = (
        P(None, ("lat", "lon")),
        P(("lat", "lon"), None),
        P(("lat", "lon")),
        P(("lat", "lon")),
        P(None, ("lat", "lon")),
        P(None, ("lat", "lon"), None, None),
        P(None, ("lat", "lon")),
        P("lat", "lon"),
        P("lat", "lon"),
        P("lat", "lon"),
        P("lat", "lon"),
        P(None, "lat", "lon"),
    )
    out_specs = (P(None, "lat", "lon"), P(None, ("lat", "lon")))
    return jax.shard_map(
        on_device, mesh=mesh, in_specs=in_specs, out_specs=out_specs, check_vma=False
    )
```

profile of v0, /device:TPU:1, one launch (start us, length us, event | category | flops | bytes accessed | tf_op | source)
XLA Modules:
  0.0 929.4 jit_solution(13546743064360122939)
XLA Ops:
  3.3 9.5 %all-to-all-start.2 = ((s32[1,16,2]{2,0,1:T(1,128)}), s32[1,16,2]{2,0,1:T(1,128)}, u32[]{:S(2)}, u32[]{:S(2)}) async-start(s32[1,16,2]{2,0,1:T(1,128)} %bitcast.19), calls=%async_computation.2 | async-start | bytes 16384 | tf_op jit(solution)/shard_map/all_to_all | solution.py:86
  34.0 10.6 %all-to-all-start = ((s32[1,128,8]{2,0,1:T(1,128)}), s32[1,128,8]{2,0,1:T(1,128)S(1)}, u32[]{:S(2)}, u32[]{:S(2)}) async-start(s32[1,128,8]{2,0,1:T(1,128)} %bitcast.170), calls=%async_computation | async-start | bytes 131072 | tf_op jit(solution)/shard_map/all_to_all | solution.py:108
  46.6 7.7 all-to-all-done
  60.5 8.2 all-to-all-done.1
  79.1 44.3 %collective-permute-done.6 = f32[4,2,132]{1,2,0:T(8,128)S(1)} collective-permute-done((f32[4,2,132]{1,2,0:T(8,128)S(1)}, f32[4,2,132]{1,2,0:T(8,128)S(1)}, u32[]{:S(2)}, u32[]{:S(2)}) %collective-permute-start.6) | collective-permute-done | bytes 4256 | tf_op jit(solution)/shard_map/ppermute | solution.py:17
  137.0 29.1 %scatter_custom_fusion.2 = f32[25,32768]{0,1:T(8,128)} fusion(s32[4096]{0:T(1024)S(1)} %bitcast.174, f32[4096,25]{1,0:T(8,128)S(1)} %copy.121, f32[]{:T(128)} %constant.8.clone.1), kind=kCustom, calls=%fused_computation.34 | custom fusion | flops 102400 | bytes 3276804 | tf_op jit(solution)/shard_map/scatter-add | solution.py:120
  166.1 13.8 %copy.124 = f32[25,256,128]{1,2,0:T(8,128)} copy(f32[25,256,128]{0,2,1:T(8,128)} %bitcast.142) | data formatting | bytes 6553600 | tf_op jit(solution)/shard_map/reshape | solution.py:122
  180.5 5.0 scatter_fusion
  193.2 662.8 %while.10 = (s32[]{:T(128)}, f32[25,256,128]{1,2,0:T(8,128)S(1)}, f32[1,256,128]{1,2,0:T(8,128)}, f32[1,256,128]{1,2,0:T(8,128)S(1)}, f32[1,256,128]{1,2,0:T(8,1...) while((s32[]{:T(128)}, f32[25,256,128]{1,2,0:T(8,128)S(1)}, ...), condition=%wide.region_8.9_spmd, body=%wide.region_7.8_spmd.sunk | while | flops 20622068 | bytes 71233680 | solution.py:134
  194.3 6.1 collective-permute-start.1
  213.2 5.4 collective-permute-start.3
  225.3 14.4 %pad_maximum_fusion.15 = (f32[25,257,130]{2,1,0:T(8,128)}, f32[25,257,130]{2,1,0:T(8,128)}) fusion(f32[25,1,130]{2,1,0:T(1,128)} %collective-permute-done.2, f32[25,256,1]{2,1,0:T(8,128)} %copy.159, f32[25,256,128]{2,1,0:T(8,128)S(1)} %copy.160, f32[25,256,1]{2,1,0:T(8,128)} %copy.161, f32[25,1,130]{2,1,0:T(1,128)} %collective-permute-done.3), kind=kLoop, calls=%fused_computation.9.clone.1 | loop fusion | flops 5011500 | bytes 10036000 | tf_op jit(solution)/shard_map/while/body/eval_jaxpr/concatenate | solution.py:15
  239.7 17.5 %fusion.46 = f32[25,256,128]{2,1,0:T(8,128)} fusion(f32[25,257,130]{2,1,0:T(8,128)} %get-tuple-element.182, f32[25,257,130]{2,1,0:T(8,128)} %get-tuple-element.183, f32[25,256,128]{2,1,0:T(8,128)S(1)} %copy.160, f32[25,256,1]{2,1,0:T(8,128)} %copy.161, f32[25,256,1]{2,1,0:T(8,128)} %copy.159, f32[256,128]{1,0:T(8,128)} %copy.162, ...), kind=kLoop, calls=%fused_computation.13.clone.1 | loop fusion | flops 15564800 | bytes 26920960 | tf_op jit(solution)/shard_map/while/body/eval_jaxpr/add | solution.py:56
  276.4 5.2 collective-permute-start.3
  288.3 14.4 %pad_maximum_fusion.15 = (f32[25,257,130]{2,1,0:T(8,128)}, f32[25,257,130]{2,1,0:T(8,128)}) fusion(f32[25,1,130]{2,1,0:T(1,128)} %collective-permute-done.2, f32[25,256,1]{2,1,0:T(8,128)} %copy.159, f32[25,256,128]{2,1,0:T(8,128)S(1)} %copy.160, f32[25,256,1]{2,1,0:T(8,128)} %copy.161, f32[25,1,130]{2,1,0:T(1,128)} %collective-permute-done.3), kind=kLoop, calls=%fused_computation.9.clone.1 | loop fusion | flops 5011500 | bytes 10036000 | tf_op jit(solution)/shard_map/while/body/eval_jaxpr/concatenate | solution.py:15
  302.7 17.5 %fusion.46 = f32[25,256,128]{2,1,0:T(8,128)} fusion(f32[25,257,130]{2,1,0:T(8,128)} %get-tuple-element.182, f32[25,257,130]{2,1,0:T(8,128)} %get-tuple-element.183, f32[25,256,128]{2,1,0:T(8,128)S(1)} %copy.160, f32[25,256,1]{2,1,0:T(8,128)} %copy.161, f32[25,256,1]{2,1,0:T(8,128)} %copy.159, f32[256,128]{1,0:T(8,128)} %copy.162, ...), kind=kLoop, calls=%fused_computation.13.clone.1 | loop fusion | flops 15564800 | bytes 26920960 | tf_op jit(solution)/shard_map/while/body/eval_jaxpr/add | solution.py:56
  342.2 5.2 collective-permute-start.3
  354.1 14.4 %pad_maximum_fusion.15 = (f32[25,257,130]{2,1,0:T(8,128)}, f32[25,257,130]{2,1,0:T(8,128)}) fusion(f32[25,1,130]{2,1,0:T(1,128)} %collective-permute-done.2, f32[25,256,1]{2,1,0:T(8,128)} %copy.159, f32[25,256,128]{2,1,0:T(8,128)S(1)} %copy.160, f32[25,256,1]{2,1,0:T(8,128)} %copy.161, f32[25,1,130]{2,1,0:T(1,128)} %collective-permute-done.3), kind=kLoop, calls=%fused_computation.9.clone.1 | loop fusion | flops 5011500 | bytes 10036000 | tf_op jit(solution)/shard_map/while/body/eval_jaxpr/concatenate | solution.py:15
  368.5 17.5 %fusion.46 = f32[25,256,128]{2,1,0:T(8,128)} fusion(f32[25,257,130]{2,1,0:T(8,128)} %get-tuple-element.182, f32[25,257,130]{2,1,0:T(8,128)} %get-tuple-element.183, f32[25,256,128]{2,1,0:T(8,128)S(1)} %copy.160, f32[25,256,1]{2,1,0:T(8,128)} %copy.161, f32[25,256,1]{2,1,0:T(8,128)} %copy.159, f32[256,128]{1,0:T(8,128)} %copy.162, ...), kind=kLoop, calls=%fused_computation.13.clone.1 | loop fusion | flops 15564800 | bytes 26920960 | tf_op jit(solution)/shard_map/while/body/eval_jaxpr/add | solution.py:56
  391.3 4.7 collective-permute-start
  408.8 5.2 collective-permute-start.3
  420.7 14.4 %pad_maximum_fusion.15 = (f32[25,257,130]{2,1,0:T(8,128)}, f32[25,257,130]{2,1,0:T(8,128)}) fusion(f32[25,1,130]{2,1,0:T(1,128)} %collective-permute-done.2, f32[25,256,1]{2,1,0:T(8,128)} %copy.159, f32[25,256,128]{2,1,0:T(8,128)S(1)} %copy.160, f32[25,256,1]{2,1,0:T(8,128)} %copy.161, f32[25,1,130]{2,1,0:T(1,128)} %collective-permute-done.3), kind=kLoop, calls=%fused_computation.9.clone.1 | loop fusion | flops 5011500 | bytes 10036000 | tf_op jit(solution)/shard_map/while/body/eval_jaxpr/concatenate | solution.py:15
  435.1 17.5 %fusion.46 = f32[25,256,128]{2,1,0:T(8,128)} fusion(f32[25,257,130]{2,1,0:T(8,128)} %get-tuple-element.182, f32[25,257,130]{2,1,0:T(8,128)} %get-tuple-element.183, f32[25,256,128]{2,1,0:T(8,128)S(1)} %copy.160, f32[25,256,1]{2,1,0:T(8,128)} %copy.161, f32[25,256,1]{2,1,0:T(8,128)} %copy.159, f32[256,128]{1,0:T(8,128)} %copy.162, ...), kind=kLoop, calls=%fused_computation.13.clone.1 | loop fusion | flops 15564800 | bytes 26920960 | tf_op jit(solution)/shard_map/while/body/eval_jaxpr/add | solution.py:56
  475.5 5.2 collective-permute-start.3
  487.4 14.4 %pad_maximum_fusion.15 = (f32[25,257,130]{2,1,0:T(8,128)}, f32[25,257,130]{2,1,0:T(8,128)}) fusion(f32[25,1,130]{2,1,0:T(1,128)} %collective-permute-done.2, f32[25,256,1]{2,1,0:T(8,128)} %copy.159, f32[25,256,128]{2,1,0:T(8,128)S(1)} %copy.160, f32[25,256,1]{2,1,0:T(8,128)} %copy.161, f32[25,1,130]{2,1,0:T(1,128)} %collective-permute-done.3), kind=kLoop, calls=%fused_computation.9.clone.1 | loop fusion | flops 5011500 | bytes 10036000 | tf_op jit(solution)/shard_map/while/body/eval_jaxpr/concatenate | solution.py:15
  501.8 17.5 %fusion.46 = f32[25,256,128]{2,1,0:T(8,128)} fusion(f32[25,257,130]{2,1,0:T(8,128)} %get-tuple-element.182, f32[25,257,130]{2,1,0:T(8,128)} %get-tuple-element.183, f32[25,256,128]{2,1,0:T(8,128)S(1)} %copy.160, f32[25,256,1]{2,1,0:T(8,128)} %copy.161, f32[25,256,1]{2,1,0:T(8,128)} %copy.159, f32[256,128]{1,0:T(8,128)} %copy.162, ...), kind=kLoop, calls=%fused_computation.13.clone.1 | loop fusion | flops 15564800 | bytes 26920960 | tf_op jit(solution)/shard_map/while/body/eval_jaxpr/add | solution.py:56
  542.1 5.2 collective-permute-start.3
  554.0 14.4 %pad_maximum_fusion.15 = (f32[25,257,130]{2,1,0:T(8,128)}, f32[25,257,130]{2,1,0:T(8,128)}) fusion(f32[25,1,130]{2,1,0:T(1,128)} %collective-permute-done.2, f32[25,256,1]{2,1,0:T(8,128)} %copy.159, f32[25,256,128]{2,1,0:T(8,128)S(1)} %copy.160, f32[25,256,1]{2,1,0:T(8,128)} %copy.161, f32[25,1,130]{2,1,0:T(1,128)} %collective-permute-done.3), kind=kLoop, calls=%fused_computation.9.clone.1 | loop fusion | flops 5011500 | bytes 10036000 | tf_op jit(solution)/shard_map/while/body/eval_jaxpr/concatenate | solution.py:15
  568.4 17.5 %fusion.46 = f32[25,256,128]{2,1,0:T(8,128)} fusion(f32[25,257,130]{2,1,0:T(8,128)} %get-tuple-element.182, f32[25,257,130]{2,1,0:T(8,128)} %get-tuple-element.183, f32[25,256,128]{2,1,0:T(8,128)S(1)} %copy.160, f32[25,256,1]{2,1,0:T(8,128)} %copy.161, f32[25,256,1]{2,1,0:T(8,128)} %copy.159, f32[256,128]{1,0:T(8,128)} %copy.162, ...), kind=kLoop, calls=%fused_computation.13.clone.1 | loop fusion | flops 15564800 | bytes 26920960 | tf_op jit(solution)/shard_map/while/body/eval_jaxpr/add | solution.py:56
  608.8 5.2 collective-permute-start.3
  620.7 14.4 %pad_maximum_fusion.15 = (f32[25,257,130]{2,1,0:T(8,128)}, f32[25,257,130]{2,1,0:T(8,128)}) fusion(f32[25,1,130]{2,1,0:T(1,128)} %collective-permute-done.2, f32[25,256,1]{2,1,0:T(8,128)} %copy.159, f32[25,256,128]{2,1,0:T(8,128)S(1)} %copy.160, f32[25,256,1]{2,1,0:T(8,128)} %copy.161, f32[25,1,130]{2,1,0:T(1,128)} %collective-permute-done.3), kind=kLoop, calls=%fused_computation.9.clone.1 | loop fusion | flops 5011500 | bytes 10036000 | tf_op jit(solution)/shard_map/while/body/eval_jaxpr/concatenate | solution.py:15
  635.1 17.5 %fusion.46 = f32[25,256,128]{2,1,0:T(8,128)} fusion(f32[25,257,130]{2,1,0:T(8,128)} %get-tuple-element.182, f32[25,257,130]{2,1,0:T(8,128)} %get-tuple-element.183, f32[25,256,128]{2,1,0:T(8,128)S(1)} %copy.160, f32[25,256,1]{2,1,0:T(8,128)} %copy.161, f32[25,256,1]{2,1,0:T(8,128)} %copy.159, f32[256,128]{1,0:T(8,128)} %copy.162, ...), kind=kLoop, calls=%fused_computation.13.clone.1 | loop fusion | flops 15564800 | bytes 26920960 | tf_op jit(solution)/shard_map/while/body/eval_jaxpr/add | solution.py:56
  675.4 5.2 collective-permute-start.3
  687.3 14.4 %pad_maximum_fusion.15 = (f32[25,257,130]{2,1,0:T(8,128)}, f32[25,257,130]{2,1,0:T(8,128)}) fusion(f32[25,1,130]{2,1,0:T(1,128)} %collective-permute-done.2, f32[25,256,1]{2,1,0:T(8,128)} %copy.159, f32[25,256,128]{2,1,0:T(8,128)S(1)} %copy.160, f32[25,256,1]{2,1,0:T(8,128)} %copy.161, f32[25,1,130]{2,1,0:T(1,128)} %collective-permute-done.3), kind=kLoop, calls=%fused_computation.9.clone.1 | loop fusion | flops 5011500 | bytes 10036000 | tf_op jit(solution)/shard_map/while/body/eval_jaxpr/concatenate | solution.py:15
  701.7 17.5 %fusion.46 = f32[25,256,128]{2,1,0:T(8,128)} fusion(f32[25,257,130]{2,1,0:T(8,128)} %get-tuple-element.182, f32[25,257,130]{2,1,0:T(8,128)} %get-tuple-element.183, f32[25,256,128]{2,1,0:T(8,128)S(1)} %copy.160, f32[25,256,1]{2,1,0:T(8,128)} %copy.161, f32[25,256,1]{2,1,0:T(8,128)} %copy.159, f32[256,128]{1,0:T(8,128)} %copy.162, ...), kind=kLoop, calls=%fused_computation.13.clone.1 | loop fusion | flops 15564800 | bytes 26920960 | tf_op jit(solution)/shard_map/while/body/eval_jaxpr/add | solution.py:56
  742.0 5.2 collective-permute-start.3
  753.9 14.4 %pad_maximum_fusion.15 = (f32[25,257,130]{2,1,0:T(8,128)}, f32[25,257,130]{2,1,0:T(8,128)}) fusion(f32[25,1,130]{2,1,0:T(1,128)} %collective-permute-done.2, f32[25,256,1]{2,1,0:T(8,128)} %copy.159, f32[25,256,128]{2,1,0:T(8,128)S(1)} %copy.160, f32[25,256,1]{2,1,0:T(8,128)} %copy.161, f32[25,1,130]{2,1,0:T(1,128)} %collective-permute-done.3), kind=kLoop, calls=%fused_computation.9.clone.1 | loop fusion | flops 5011500 | bytes 10036000 | tf_op jit(solution)/shard_map/while/body/eval_jaxpr/concatenate | solution.py:15
  768.3 17.5 %fusion.46 = f32[25,256,128]{2,1,0:T(8,128)} fusion(f32[25,257,130]{2,1,0:T(8,128)} %get-tuple-element.182, f32[25,257,130]{2,1,0:T(8,128)} %get-tuple-element.183, f32[25,256,128]{2,1,0:T(8,128)S(1)} %copy.160, f32[25,256,1]{2,1,0:T(8,128)} %copy.161, f32[25,256,1]{2,1,0:T(8,128)} %copy.159, f32[256,128]{1,0:T(8,128)} %copy.162, ...), kind=kLoop, calls=%fused_computation.13.clone.1 | loop fusion | flops 15564800 | bytes 26920960 | tf_op jit(solution)/shard_map/while/body/eval_jaxpr/add | solution.py:56
  791.1 4.7 collective-permute-start
  808.7 5.2 collective-permute-start.3
  820.6 14.4 %pad_maximum_fusion.15 = (f32[25,257,130]{2,1,0:T(8,128)}, f32[25,257,130]{2,1,0:T(8,128)}) fusion(f32[25,1,130]{2,1,0:T(1,128)} %collective-permute-done.2, f32[25,256,1]{2,1,0:T(8,128)} %copy.159, f32[25,256,128]{2,1,0:T(8,128)S(1)} %copy.160, f32[25,256,1]{2,1,0:T(8,128)} %copy.161, f32[25,1,130]{2,1,0:T(1,128)} %collective-permute-done.3), kind=kLoop, calls=%fused_computation.9.clone.1 | loop fusion | flops 5011500 | bytes 10036000 | tf_op jit(solution)/shard_map/while/body/eval_jaxpr/concatenate | solution.py:15
  835.0 17.5 %fusion.46 = f32[25,256,128]{2,1,0:T(8,128)} fusion(f32[25,257,130]{2,1,0:T(8,128)} %get-tuple-element.182, f32[25,257,130]{2,1,0:T(8,128)} %get-tuple-element.183, f32[25,256,128]{2,1,0:T(8,128)S(1)} %copy.160, f32[25,256,1]{2,1,0:T(8,128)} %copy.161, f32[25,256,1]{2,1,0:T(8,128)} %copy.159, f32[256,128]{1,0:T(8,128)} %copy.162, ...), kind=kLoop, calls=%fused_computation.13.clone.1 | loop fusion | flops 15564800 | bytes 26920960 | tf_op jit(solution)/shard_map/while/body/eval_jaxpr/add | solution.py:56
  862.4 9.0 copy.133
  871.5 8.6 gather_fusion.3
  880.1 8.6 gather_fusion.2
  888.7 8.6 gather_fusion.1
  897.3 8.6 gather_fusion
  906.9 19.4 %all_to_all.41 = f32[128,1,200]{2,1,0:T(1,128)S(1)} all-to-all(f32[128,1,200]{2,1,0:T(1,128)S(1)} %reshape.502), channel_id=1, replica_groups=mesh['lat'=8,'lon'=16] {'lat','lon'}, dimensions={0} | all-to-all | bytes 204800 | tf_op jit(solution)/shard_map/all_to_all | solution.py:143
  (449 shorter events, 349.4 us)
Async XLA Ops:
  3.3 30.7 %all-to-all-start.2 = ((s32[1,16,2]{2,0,1:T(1,128)}), s32[1,16,2]{2,0,1:T(1,128)}, u32[]{:S(2)}, u32[]{:S(2)}) async-start(s32[1,16,2]{2,0,1:T(1,128)} %bitcast.19), calls=%async_computation.2 | async-start | bytes 16384 | tf_op jit(solution)/shard_map/all_to_all | solution.py:86
  17.5 57.0 %collective-permute-start.4 = (f32[4,256,2]{1,2,0:T(2,128)}, f32[4,256,2]{1,2,0:T(2,128)S(1)}, u32[]{:S(2)}, u32[]{:S(2)}) collective-permute-start(f32[4,256,2]{1,2,0:T(2,128)} %get-tuple-element.95), channel_id=1, source_target_pairs={{0,1},{1,2},{2,3},{3,4},{4,5},{5,6},{6,7},{7,8},{8,9},{9,10},{10,1... | collective-permute-start | bytes 24584 | tf_op jit(solution)/shard_map/ppermute | solution.py:17
  19.2 55.4 %collective-permute-start.5 = (f32[4,256,2]{1,2,0:T(2,128)}, f32[4,256,2]{1,2,0:T(2,128)S(1)}, u32[]{:S(2)}, u32[]{:S(2)}) collective-permute-start(f32[4,256,2]{1,2,0:T(2,128)} %get-tuple-element.96), channel_id=1, source_target_pairs={{1,0},{2,1},{3,2},{4,3},{5,4},{6,5},{7,6},{8,7},{9,8},{10,9},{11,1... | collective-permute-start | bytes 24584 | tf_op jit(solution)/shard_map/ppermute | solution.py:19
  34.0 20.3 %all-to-all-start = ((s32[1,128,8]{2,0,1:T(1,128)}), s32[1,128,8]{2,0,1:T(1,128)S(1)}, u32[]{:S(2)}, u32[]{:S(2)}) async-start(s32[1,128,8]{2,0,1:T(1,128)} %bitcast.170), calls=%async_computation | async-start | bytes 131072 | tf_op jit(solution)/shard_map/all_to_all | solution.py:108
  54.3 14.4 %all-to-all-start.1 = ((f32[128,1,232]{2,1,0:T(1,128)}), f32[128,1,232]{2,1,0:T(1,128)S(1)}, u32[]{:S(2)}, u32[]{:S(2)}) async-start(f32[128,1,232]{2,1,0:T(1,128)} %reshape.500), calls=%async_computation.1 | async-start | bytes 262144 | tf_op jit(solution)/shard_map/all_to_all | solution.py:107
  68.7 111.1 %all-to-all-start.3 = ((f32[25,32,8,128]{3,2,0,1:T(8,128)}), f32[25,32,8,128]{3,2,0,1:T(8,128)}, u32[]{:S(2)}, u32[]{:S(2)}) async-start(f32[25,32,8,128]{3,2,0,1:T(8,128)} %copy.123), calls=%async_computation.3 | async-start | bytes 6553600 | tf_op jit(solution)/shard_map/all_to_all | solution.py:85
  74.8 48.7 %collective-permute-start.6 = (f32[4,2,132]{1,2,0:T(8,128)S(1)}, f32[4,2,132]{1,2,0:T(8,128)S(1)}, u32[]{:S(2)}, u32[]{:S(2)}) collective-permute-start(f32[4,2,132]{1,2,0:T(8,128)S(1)} %get-tuple-element.89), channel_id=1, source_target_pairs={{0,16},{16,32},{32,48},{48,64},{64,80},{80,96},{96,112},{1,17},{17... | collective-permute-start | bytes 12680 | tf_op jit(solution)/shard_map/ppermute | solution.py:17
  77.1 46.4 %collective-permute-start.7 = (f32[4,2,132]{1,2,0:T(8,128)S(1)}, f32[4,2,132]{1,2,0:T(8,128)S(1)}, u32[]{:S(2)}, u32[]{:S(2)}) collective-permute-start(f32[4,2,132]{1,2,0:T(8,128)S(1)} %get-tuple-element.90), channel_id=1, source_target_pairs={{16,0},{32,16},{48,32},{64,48},{80,64},{96,80},{112,96},{17,1},{33... | collective-permute-start | bytes 12680 | tf_op jit(solution)/shard_map/ppermute | solution.py:19
  194.3 9.8 %collective-permute-start.1 = (f32[25,256,1]{1,2,0:T(1,128)}, f32[25,256,1]{1,2,0:T(1,128)}, u32[]{:S(2)}, u32[]{:S(2)}) collective-permute-start(f32[25,256,1]{1,2,0:T(1,128)} %get-tuple-element.179), channel_id=1, source_target_pairs={{0,1},{1,2},{2,3},{3,4},{4,5},{5,6},{6,7},{7,8},{8,9},{9,10},{10,1... | collective-permute-start | bytes 76808 | tf_op jit(solution)/shard_map/while/body/eval_jaxpr/ppermute | solution.py:17
  200.4 6.7 collective-permute-start
  211.9 13.3 %collective-permute-start.2 = (f32[25,1,130]{2,1,0:T(1,128)}, f32[25,1,130]{2,1,0:T(1,128)}, u32[]{:S(2)}, u32[]{:S(2)}) collective-permute-start(f32[25,1,130]{2,1,0:T(1,128)} %get-tuple-element.180), channel_id=1, source_target_pairs={{16,0},{32,16},{48,32},{64,48},{80,64},{96,80},{112,96},{17,1},{33... | collective-permute-start | bytes 39008 | tf_op jit(solution)/shard_map/while/body/eval_jaxpr/ppermute | solution.py:19
  213.2 12.1 %collective-permute-start.3 = (f32[25,1,130]{2,1,0:T(1,128)}, f32[25,1,130]{2,1,0:T(1,128)}, u32[]{:S(2)}, u32[]{:S(2)}) collective-permute-start(f32[25,1,130]{2,1,0:T(1,128)} %get-tuple-element.181), channel_id=1, source_target_pairs={{0,16},{16,32},{32,48},{48,64},{64,80},{80,96},{96,112},{1,17},{17... | collective-permute-start | bytes 39008 | tf_op jit(solution)/shard_map/while/body/eval_jaxpr/ppermute | solution.py:17
  261.6 5.7 collective-permute-start.1
  263.6 6.7 collective-permute-start
  275.1 13.2 %collective-permute-start.2 = (f32[25,1,130]{2,1,0:T(1,128)}, f32[25,1,130]{2,1,0:T(1,128)}, u32[]{:S(2)}, u32[]{:S(2)}) collective-permute-start(f32[25,1,130]{2,1,0:T(1,128)} %get-tuple-element.180), channel_id=1, source_target_pairs={{16,0},{32,16},{48,32},{64,48},{80,64},{96,80},{112,96},{17,1},{33... | collective-permute-start | bytes 39008 | tf_op jit(solution)/shard_map/while/body/eval_jaxpr/ppermute | solution.py:19
  276.4 11.9 %collective-permute-start.3 = (f32[25,1,130]{2,1,0:T(1,128)}, f32[25,1,130]{2,1,0:T(1,128)}, u32[]{:S(2)}, u32[]{:S(2)}) collective-permute-start(f32[25,1,130]{2,1,0:T(1,128)} %get-tuple-element.181), channel_id=1, source_target_pairs={{0,16},{16,32},{32,48},{48,64},{64,80},{80,96},{96,112},{1,17},{17... | collective-permute-start | bytes 39008 | tf_op jit(solution)/shard_map/while/body/eval_jaxpr/ppermute | solution.py:17
  324.6 8.4 collective-permute-start.1
  326.6 9.4 %collective-permute-start = (f32[25,256,1]{1,2,0:T(1,128)}, f32[25,256,1]{1,2,0:T(1,128)}, u32[]{:S(2)}, u32[]{:S(2)}) collective-permute-start(f32[25,256,1]{1,2,0:T(1,128)} %get-tuple-element.178), channel_id=1, source_target_pairs={{1,0},{2,1},{3,2},{4,3},{5,4},{6,5},{7,6},{8,7},{9,8},{10,9},{11,1... | collective-permute-start | bytes 76808 | tf_op jit(solution)/shard_map/while/body/eval_jaxpr/ppermute | solution.py:19
  340.9 13.2 %collective-permute-start.2 = (f32[25,1,130]{2,1,0:T(1,128)}, f32[25,1,130]{2,1,0:T(1,128)}, u32[]{:S(2)}, u32[]{:S(2)}) collective-permute-start(f32[25,1,130]{2,1,0:T(1,128)} %get-tuple-element.180), channel_id=1, source_target_pairs={{16,0},{32,16},{48,32},{64,48},{80,64},{96,80},{112,96},{17,1},{33... | collective-permute-start | bytes 39008 | tf_op jit(solution)/shard_map/while/body/eval_jaxpr/ppermute | solution.py:19
  342.2 11.9 %collective-permute-start.3 = (f32[25,1,130]{2,1,0:T(1,128)}, f32[25,1,130]{2,1,0:T(1,128)}, u32[]{:S(2)}, u32[]{:S(2)}) collective-permute-start(f32[25,1,130]{2,1,0:T(1,128)} %get-tuple-element.181), channel_id=1, source_target_pairs={{0,16},{16,32},{32,48},{48,64},{64,80},{80,96},{96,112},{1,17},{17... | collective-permute-start | bytes 39008 | tf_op jit(solution)/shard_map/while/body/eval_jaxpr/ppermute | solution.py:17
  390.4 9.3 %collective-permute-start.1 = (f32[25,256,1]{1,2,0:T(1,128)}, f32[25,256,1]{1,2,0:T(1,128)}, u32[]{:S(2)}, u32[]{:S(2)}) collective-permute-start(f32[25,256,1]{1,2,0:T(1,128)} %get-tuple-element.179), channel_id=1, source_target_pairs={{0,1},{1,2},{2,3},{3,4},{4,5},{5,6},{6,7},{7,8},{8,9},{9,10},{10,1... | collective-permute-start | bytes 76808 | tf_op jit(solution)/shard_map/while/body/eval_jaxpr/ppermute | solution.py:17
  391.3 11.4 %collective-permute-start = (f32[25,256,1]{1,2,0:T(1,128)}, f32[25,256,1]{1,2,0:T(1,128)}, u32[]{:S(2)}, u32[]{:S(2)}) collective-permute-start(f32[25,256,1]{1,2,0:T(1,128)} %get-tuple-element.178), channel_id=1, source_target_pairs={{1,0},{2,1},{3,2},{4,3},{5,4},{6,5},{7,6},{8,7},{9,8},{10,9},{11,1... | collective-permute-start | bytes 76808 | tf_op jit(solution)/shard_map/while/body/eval_jaxpr/ppermute | solution.py:19
  407.5 13.2 %collective-permute-start.2 = (f32[25,1,130]{2,1,0:T(1,128)}, f32[25,1,130]{2,1,0:T(1,128)}, u32[]{:S(2)}, u32[]{:S(2)}) collective-permute-start(f32[25,1,130]{2,1,0:T(1,128)} %get-tuple-element.180), channel_id=1, source_target_pairs={{16,0},{32,16},{48,32},{64,48},{80,64},{96,80},{112,96},{17,1},{33... | collective-permute-start | bytes 39008 | tf_op jit(solution)/shard_map/while/body/eval_jaxpr/ppermute | solution.py:19
  408.8 11.9 %collective-permute-start.3 = (f32[25,1,130]{2,1,0:T(1,128)}, f32[25,1,130]{2,1,0:T(1,128)}, u32[]{:S(2)}, u32[]{:S(2)}) collective-permute-start(f32[25,1,130]{2,1,0:T(1,128)} %get-tuple-element.181), channel_id=1, source_target_pairs={{0,16},{16,32},{32,48},{48,64},{64,80},{80,96},{96,112},{1,17},{17... | collective-permute-start | bytes 39008 | tf_op jit(solution)/shard_map/while/body/eval_jaxpr/ppermute | solution.py:17
  457.0 9.3 %collective-permute-start.1 = (f32[25,256,1]{1,2,0:T(1,128)}, f32[25,256,1]{1,2,0:T(1,128)}, u32[]{:S(2)}, u32[]{:S(2)}) collective-permute-start(f32[25,256,1]{1,2,0:T(1,128)} %get-tuple-element.179), channel_id=1, source_target_pairs={{0,1},{1,2},{2,3},{3,4},{4,5},{5,6},{6,7},{7,8},{8,9},{9,10},{10,1... | collective-permute-start | bytes 76808 | tf_op jit(solution)/shard_map/while/body/eval_jaxpr/ppermute | solution.py:17
  457.9 11.4 %collective-permute-start = (f32[25,256,1]{1,2,0:T(1,128)}, f32[25,256,1]{1,2,0:T(1,128)}, u32[]{:S(2)}, u32[]{:S(2)}) collective-permute-start(f32[25,256,1]{1,2,0:T(1,128)} %get-tuple-element.178), channel_id=1, source_target_pairs={{1,0},{2,1},{3,2},{4,3},{5,4},{6,5},{7,6},{8,7},{9,8},{10,9},{11,1... | collective-permute-start | bytes 76808 | tf_op jit(solution)/shard_map/while/body/eval_jaxpr/ppermute | solution.py:19
  474.2 13.2 %collective-permute-start.2 = (f32[25,1,130]{2,1,0:T(1,128)}, f32[25,1,130]{2,1,0:T(1,128)}, u32[]{:S(2)}, u32[]{:S(2)}) collective-permute-start(f32[25,1,130]{2,1,0:T(1,128)} %get-tuple-element.180), channel_id=1, source_target_pairs={{16,0},{32,16},{48,32},{64,48},{80,64},{96,80},{112,96},{17,1},{33... | collective-permute-start | bytes 39008 | tf_op jit(solution)/shard_map/while/body/eval_jaxpr/ppermute | solution.py:19
  475.5 11.9 %collective-permute-start.3 = (f32[25,1,130]{2,1,0:T(1,128)}, f32[25,1,130]{2,1,0:T(1,128)}, u32[]{:S(2)}, u32[]{:S(2)}) collective-permute-start(f32[25,1,130]{2,1,0:T(1,128)} %get-tuple-element.181), channel_id=1, source_target_pairs={{0,16},{16,32},{32,48},{48,64},{64,80},{80,96},{96,112},{1,17},{17... | collective-permute-start | bytes 39008 | tf_op jit(solution)/shard_map/while/body/eval_jaxpr/ppermute | solution.py:17
  523.6 9.3 %collective-permute-start.1 = (f32[25,256,1]{1,2,0:T(1,128)}, f32[25,256,1]{1,2,0:T(1,128)}, u32[]{:S(2)}, u32[]{:S(2)}) collective-permute-start(f32[25,256,1]{1,2,0:T(1,128)} %get-tuple-element.179), channel_id=1, source_target_pairs={{0,1},{1,2},{2,3},{3,4},{4,5},{5,6},{6,7},{7,8},{8,9},{9,10},{10,1... | collective-permute-start | bytes 76808 | tf_op jit(solution)/shard_map/while/body/eval_jaxpr/ppermute | solution.py:17
  524.6 11.4 %collective-permute-start = (f32[25,256,1]{1,2,0:T(1,128)}, f32[25,256,1]{1,2,0:T(1,128)}, u32[]{:S(2)}, u32[]{:S(2)}) collective-permute-start(f32[25,256,1]{1,2,0:T(1,128)} %get-tuple-element.178), channel_id=1, source_target_pairs={{1,0},{2,1},{3,2},{4,3},{5,4},{6,5},{7,6},{8,7},{9,8},{10,9},{11,1... | collective-permute-start | bytes 76808 | tf_op jit(solution)/shard_map/while/body/eval_jaxpr/ppermute | solution.py:19
  540.8 13.2 %collective-permute-start.2 = (f32[25,1,130]{2,1,0:T(1,128)}, f32[25,1,130]{2,1,0:T(1,128)}, u32[]{:S(2)}, u32[]{:S(2)}) collective-permute-start(f32[25,1,130]{2,1,0:T(1,128)} %get-tuple-element.180), channel_id=1, source_target_pairs={{16,0},{32,16},{48,32},{64,48},{80,64},{96,80},{112,96},{17,1},{33... | collective-permute-start | bytes 39008 | tf_op jit(solution)/shard_map/while/body/eval_jaxpr/ppermute | solution.py:19
  542.1 11.9 %collective-permute-start.3 = (f32[25,1,130]{2,1,0:T(1,128)}, f32[25,1,130]{2,1,0:T(1,128)}, u32[]{:S(2)}, u32[]{:S(2)}) collective-permute-start(f32[25,1,130]{2,1,0:T(1,128)} %get-tuple-element.181), channel_id=1, source_target_pairs={{0,16},{16,32},{32,48},{48,64},{64,80},{80,96},{96,112},{1,17},{17... | collective-permute-start | bytes 39008 | tf_op jit(solution)/shard_map/while/body/eval_jaxpr/ppermute | solution.py:17
  590.3 9.3 %collective-permute-start.1 = (f32[25,256,1]{1,2,0:T(1,128)}, f32[25,256,1]{1,2,0:T(1,128)}, u32[]{:S(2)}, u32[]{:S(2)}) collective-permute-start(f32[25,256,1]{1,2,0:T(1,128)} %get-tuple-element.179), channel_id=1, source_target_pairs={{0,1},{1,2},{2,3},{3,4},{4,5},{5,6},{6,7},{7,8},{8,9},{9,10},{10,1... | collective-permute-start | bytes 76808 | tf_op jit(solution)/shard_map/while/body/eval_jaxpr/ppermute | solution.py:17
  591.2 11.4 %collective-permute-start = (f32[25,256,1]{1,2,0:T(1,128)}, f32[25,256,1]{1,2,0:T(1,128)}, u32[]{:S(2)}, u32[]{:S(2)}) collective-permute-start(f32[25,256,1]{1,2,0:T(1,128)} %get-tuple-element.178), channel_id=1, source_target_pairs={{1,0},{2,1},{3,2},{4,3},{5,4},{6,5},{7,6},{8,7},{9,8},{10,9},{11,1... | collective-permute-start | bytes 76808 | tf_op jit(solution)/shard_map/while/body/eval_jaxpr/ppermute | solution.py:19
  607.5 13.2 %collective-permute-start.2 = (f32[25,1,130]{2,1,0:T(1,128)}, f32[25,1,130]{2,1,0:T(1,128)}, u32[]{:S(2)}, u32[]{:S(2)}) collective-permute-start(f32[25,1,130]{2,1,0:T(1,128)} %get-tuple-element.180), channel_id=1, source_target_pairs={{16,0},{32,16},{48,32},{64,48},{80,64},{96,80},{112,96},{17,1},{33... | collective-permute-start | bytes 39008 | tf_op jit(solution)/shard_map/while/body/eval_jaxpr/ppermute | solution.py:19
  608.8 11.9 %collective-permute-start.3 = (f32[25,1,130]{2,1,0:T(1,128)}, f32[25,1,130]{2,1,0:T(1,128)}, u32[]{:S(2)}, u32[]{:S(2)}) collective-permute-start(f32[25,1,130]{2,1,0:T(1,128)} %get-tuple-element.181), channel_id=1, source_target_pairs={{0,16},{16,32},{32,48},{48,64},{64,80},{80,96},{96,112},{1,17},{17... | collective-permute-start | bytes 39008 | tf_op jit(solution)/shard_map/while/body/eval_jaxpr/ppermute | solution.py:17
  656.9 9.3 %collective-permute-start.1 = (f32[25,256,1]{1,2,0:T(1,128)}, f32[25,256,1]{1,2,0:T(1,128)}, u32[]{:S(2)}, u32[]{:S(2)}) collective-permute-start(f32[25,256,1]{1,2,0:T(1,128)} %get-tuple-element.179), channel_id=1, source_target_pairs={{0,1},{1,2},{2,3},{3,4},{4,5},{5,6},{6,7},{7,8},{8,9},{9,10},{10,1... | collective-permute-start | bytes 76808 | tf_op jit(solution)/shard_map/while/body/eval_jaxpr/ppermute | solution.py:17
  657.9 11.4 %collective-permute-start = (f32[25,256,1]{1,2,0:T(1,128)}, f32[25,256,1]{1,2,0:T(1,128)}, u32[]{:S(2)}, u32[]{:S(2)}) collective-permute-start(f32[25,256,1]{1,2,0:T(1,128)} %get-tuple-element.178), channel_id=1, source_target_pairs={{1,0},{2,1},{3,2},{4,3},{5,4},{6,5},{7,6},{8,7},{9,8},{10,9},{11,1... | collective-permute-start | bytes 76808 | tf_op jit(solution)/shard_map/while/body/eval_jaxpr/ppermute | solution.py:19
  674.1 13.2 %collective-permute-start.2 = (f32[25,1,130]{2,1,0:T(1,128)}, f32[25,1,130]{2,1,0:T(1,128)}, u32[]{:S(2)}, u32[]{:S(2)}) collective-permute-start(f32[25,1,130]{2,1,0:T(1,128)} %get-tuple-element.180), channel_id=1, source_target_pairs={{16,0},{32,16},{48,32},{64,48},{80,64},{96,80},{112,96},{17,1},{33... | collective-permute-start | bytes 39008 | tf_op jit(solution)/shard_map/while/body/eval_jaxpr/ppermute | solution.py:19
  675.4 11.9 %collective-permute-start.3 = (f32[25,1,130]{2,1,0:T(1,128)}, f32[25,1,130]{2,1,0:T(1,128)}, u32[]{:S(2)}, u32[]{:S(2)}) collective-permute-start(f32[25,1,130]{2,1,0:T(1,128)} %get-tuple-element.181), channel_id=1, source_target_pairs={{0,16},{16,32},{32,48},{48,64},{64,80},{80,96},{96,112},{1,17},{17... | collective-permute-start | bytes 39008 | tf_op jit(solution)/shard_map/while/body/eval_jaxpr/ppermute | solution.py:17
  723.6 9.3 %collective-permute-start.1 = (f32[25,256,1]{1,2,0:T(1,128)}, f32[25,256,1]{1,2,0:T(1,128)}, u32[]{:S(2)}, u32[]{:S(2)}) collective-permute-start(f32[25,256,1]{1,2,0:T(1,128)} %get-tuple-element.179), channel_id=1, source_target_pairs={{0,1},{1,2},{2,3},{3,4},{4,5},{5,6},{6,7},{7,8},{8,9},{9,10},{10,1... | collective-permute-start | bytes 76808 | tf_op jit(solution)/shard_map/while/body/eval_jaxpr/ppermute | solution.py:17
  724.5 11.4 %collective-permute-start = (f32[25,256,1]{1,2,0:T(1,128)}, f32[25,256,1]{1,2,0:T(1,128)}, u32[]{:S(2)}, u32[]{:S(2)}) collective-permute-start(f32[25,256,1]{1,2,0:T(1,128)} %get-tuple-element.178), channel_id=1, source_target_pairs={{1,0},{2,1},{3,2},{4,3},{5,4},{6,5},{7,6},{8,7},{9,8},{10,9},{11,1... | collective-permute-start | bytes 76808 | tf_op jit(solution)/shard_map/while/body/eval_jaxpr/ppermute | solution.py:19
  740.7 13.2 %collective-permute-start.2 = (f32[25,1,130]{2,1,0:T(1,128)}, f32[25,1,130]{2,1,0:T(1,128)}, u32[]{:S(2)}, u32[]{:S(2)}) collective-permute-start(f32[25,1,130]{2,1,0:T(1,128)} %get-tuple-element.180), channel_id=1, source_target_pairs={{16,0},{32,16},{48,32},{64,48},{80,64},{96,80},{112,96},{17,1},{33... | collective-permute-start | bytes 39008 | tf_op jit(solution)/shard_map/while/body/eval_jaxpr/ppermute | solution.py:19
  742.0 11.9 %collective-permute-start.3 = (f32[25,1,130]{2,1,0:T(1,128)}, f32[25,1,130]{2,1,0:T(1,128)}, u32[]{:S(2)}, u32[]{:S(2)}) collective-permute-start(f32[25,1,130]{2,1,0:T(1,128)} %get-tuple-element.181), channel_id=1, source_target_pairs={{0,16},{16,32},{32,48},{48,64},{64,80},{80,96},{96,112},{1,17},{17... | collective-permute-start | bytes 39008 | tf_op jit(solution)/shard_map/while/body/eval_jaxpr/ppermute | solution.py:17
  790.2 9.3 %collective-permute-start.1 = (f32[25,256,1]{1,2,0:T(1,128)}, f32[25,256,1]{1,2,0:T(1,128)}, u32[]{:S(2)}, u32[]{:S(2)}) collective-permute-start(f32[25,256,1]{1,2,0:T(1,128)} %get-tuple-element.179), channel_id=1, source_target_pairs={{0,1},{1,2},{2,3},{3,4},{4,5},{5,6},{6,7},{7,8},{8,9},{9,10},{10,1... | collective-permute-start | bytes 76808 | tf_op jit(solution)/shard_map/while/body/eval_jaxpr/ppermute | solution.py:17
  791.1 11.4 %collective-permute-start = (f32[25,256,1]{1,2,0:T(1,128)}, f32[25,256,1]{1,2,0:T(1,128)}, u32[]{:S(2)}, u32[]{:S(2)}) collective-permute-start(f32[25,256,1]{1,2,0:T(1,128)} %get-tuple-element.178), channel_id=1, source_target_pairs={{1,0},{2,1},{3,2},{4,3},{5,4},{6,5},{7,6},{8,7},{9,8},{10,9},{11,1... | collective-permute-start | bytes 76808 | tf_op jit(solution)/shard_map/while/body/eval_jaxpr/ppermute | solution.py:19
  807.4 13.2 %collective-permute-start.2 = (f32[25,1,130]{2,1,0:T(1,128)}, f32[25,1,130]{2,1,0:T(1,128)}, u32[]{:S(2)}, u32[]{:S(2)}) collective-permute-start(f32[25,1,130]{2,1,0:T(1,128)} %get-tuple-element.180), channel_id=1, source_target_pairs={{16,0},{32,16},{48,32},{64,48},{80,64},{96,80},{112,96},{17,1},{33... | collective-permute-start | bytes 39008 | tf_op jit(solution)/shard_map/while/body/eval_jaxpr/ppermute | solution.py:19
  808.7 11.9 %collective-permute-start.3 = (f32[25,1,130]{2,1,0:T(1,128)}, f32[25,1,130]{2,1,0:T(1,128)}, u32[]{:S(2)}, u32[]{:S(2)}) collective-permute-start(f32[25,1,130]{2,1,0:T(1,128)} %get-tuple-element.181), channel_id=1, source_target_pairs={{0,16},{16,32},{32,48},{48,64},{64,80},{80,96},{96,112},{1,17},{17... | collective-permute-start | bytes 39008 | tf_op jit(solution)/shard_map/while/body/eval_jaxpr/ppermute | solution.py:17
  (83 other events, 953.2 us)
where the time goes:
time: 934 us; the launch traced here: 929 us
  other arithmetic  394 us (42%)
  local copies, waits for them, and re-layouts  308 us (33%)
  starting transfers between devices  145 us (16%)
  waiting for transfers between devices  60.4 us (6%)
  blocking collectives  19.4 us (2%)
    add x10, other arithmetic, advance(): centre + east_face * (padded[:, 1:-1, 2:] - centre)  175 us
    concatenate x12, other arithmetic, with_halo(): jnp.concatenate([lax.ppermute(tail, axis, [(i, (i + 1) % count) for i in...  144 us
    another operation x23, local copies, waits for them, and re-layouts  72.4 us
    ppermute x22, starting transfers between devices, with_halo(): lax.ppermute(tail, axis, [(i, (i + 1) % count) for i in range(ends)])  66.1 us
    ppermute x22, starting transfers between devices, with_halo(): lax.ppermute(head, axis, [((i + 1) % count, i) for i in range(ends)])  49.9 us
    ppermute x22, waiting for transfers between devices, with_halo(): lax.ppermute(tail, axis, [(i, (i + 1) % count) for i in range(ends)])  44.4 us
    ppermute x10, local copies, waits for them, and re-layouts, with_halo(): lax.ppermute(tail, axis, [(i, (i + 1) % count) for i in range(ends)])  29.6 us
    ppermute x10, local copies, waits for them, and re-layouts, with_halo(): lax.ppermute(head, axis, [((i + 1) % count, i) for i in range(ends)])  29.4 us
  transfers between devices with their start and end apart: 48, of which 3 were waited for; matrix products, arithmetic and copies ran while one was open for 23% of the time, Pallas kernels for 0%

commit v1 on v0

--- a/solution.py
+++ b/solution.py
@@ -140,7 +140,15 @@
         + recv_weights[2][None, :] * flat_field[:, base_cell + lon_cells]
         + recv_weights[3][None, :] * flat_field[:, base_cell + lon_cells + 1]
     )
-    returned = lax.all_to_all(sampled, ("lat", "lon"), split_axis=1, concat_axis=1, tiled=True)
+    returned = jnp.concatenate(
+        lax.all_to_all(
+            jnp.stack(jnp.split(sampled, lax.axis_size(("lat", "lon")), axis=1)),
+            ("lat", "lon"),
+            0,
+            0,
+        ),
+        axis=1,
+    )
     profile_values = returned[:, slot_of]
     return (smoothed, profile_values)
 

time: 934 us -> 896 us (0.959)
  local copies, waits for them, and re-layouts: 308 us -> 280 us
    mul x10, local copies, waits for them, and re-layouts: 0.87 us -> 16.5 us  [advance(): east_face * (padded[:, 1:-1, 2:] - centre)]
    mul x10, local copies, waits for them, and re-layouts: 16.5 us -> 0.88 us  [advance(): 0.25 * twist_face]
    another operation x23 -> x24, local copies, waits for them, and re-layouts: 72.4 us -> 72.4 us
  transfers between devices with their start and end apart: 48 -> 48, of which waited for: 3 -> 3; matrix products, arithmetic and copies ran while one was open for 23% -> 22% of each run, Pallas kernels for 0% -> 0%
where the time goes in v1:
time: 896 us; the launch traced here: 892 us
  other arithmetic  387 us (43%)
  local copies, waits for them, and re-layouts  280 us (31%)
  starting transfers between devices  139 us (16%)
  waiting for transfers between devices  60.6 us (7%)
  blocking collectives  21.8 us (2%)
    add x10, other arithmetic, advance(): centre + east_face * (padded[:, 1:-1, 2:] - centre)  175 us
    concatenate x12, other arithmetic, with_halo(): jnp.concatenate([lax.ppermute(tail, axis, [(i, (i + 1) % count) for i in...  144 us
    another operation x23, local copies, waits for them, and re-layouts  72.4 us
    ppermute x22, starting transfers between devices, with_halo(): lax.ppermute(tail, axis, [(i, (i + 1) % count) for i in range(ends)])  60.1 us
    ppermute x22, starting transfers between devices, with_halo(): lax.ppermute(head, axis, [((i + 1) % count, i) for i in range(ends)])  52.6 us
    ppermute x22, waiting for transfers between devices, with_halo(): lax.ppermute(tail, axis, [(i, (i + 1) % count) for i in range(ends)])  44.4 us
    scatter-add x1, other arithmetic, on_device(): jnp.zeros((levels, lat_cells * lon_cells), jnp.float32).at[:, corner_cells]  29.1 us
    ppermute x10, local copies, waits for them, and re-layouts, with_halo(): lax.ppermute(tail, axis, [(i, (i + 1) % count) for i in range(ends)])  23.4 us
  transfers between devices with their start and end apart: 48, of which 3 were waited for; matrix products, arithmetic and copies ran while one was open for 22% of the time, Pallas kernels for 0%

profile of v1, /device:TPU:1, one launch (start us, length us, event | category | flops | bytes accessed | tf_op | source)
XLA Modules:
  0.0 892.5 jit_solution(15531985250861903136)
XLA Ops:
  10.9 8.3 all-to-all-start.2
  34.1 9.3 %all-to-all-start = ((s32[1,128,8]{2,0,1:T(1,128)}), s32[1,128,8]{2,0,1:T(1,128)S(1)}, u32[]{:S(2)}, u32[]{:S(2)}) async-start(s32[1,128,8]{2,0,1:T(1,128)} %bitcast.635), calls=%async_computation | async-start | bytes 131072 | tf_op jit(solution)/shard_map/all_to_all | solution.py:108
  45.4 7.8 all-to-all-done
  59.2 8.4 all-to-all-done.1
  67.6 4.6 all-to-all-start.3
  78.0 44.3 %collective-permute-done.6 = f32[4,2,132]{1,2,0:T(8,128)S(1)} collective-permute-done((f32[4,2,132]{1,2,0:T(8,128)S(1)}, f32[4,2,132]{1,2,0:T(8,128)S(1)}, u32[]{:S(2)}, u32[]{:S(2)}) %collective-permute-start.6) | collective-permute-done | bytes 4256 | tf_op jit(solution)/shard_map/ppermute | solution.py:17
  130.0 29.1 %scatter_custom_fusion.2 = f32[25,32768]{0,1:T(8,128)} fusion(s32[4096]{0:T(1024)S(1)} %bitcast.639, f32[4096,25]{1,0:T(8,128)S(1)} %copy.553, f32[]{:T(128)} %constant.8.clone.1), kind=kCustom, calls=%fused_computation.34 | custom fusion | flops 102400 | bytes 3276804 | tf_op jit(solution)/shard_map/scatter-add | solution.py:120
  159.2 13.8 %copy.556 = f32[25,256,128]{1,2,0:T(8,128)} copy(f32[25,256,128]{0,2,1:T(8,128)} %bitcast.610) | data formatting | bytes 6553600 | tf_op jit(solution)/shard_map/reshape | solution.py:122
  173.6 5.0 scatter_fusion
  186.4 628.8 %while.10 = (s32[]{:T(128)}, f32[25,256,128]{1,2,0:T(8,128)S(1)}, f32[1,256,128]{1,2,0:T(8,128)}, f32[1,256,128]{1,2,0:T(8,128)}, f32[1,256,128]{1,2,0:T(8,128)}...) while((s32[]{:T(128)}, f32[25,256,128]{1,2,0:T(8,128)S(1)}, f32[1,256,128]{1,2,0:T(8,128)}, ...), condition=%wide.region_8.9_spmd, body=%wide.region_7.8_spmd.sunk | while | flops 20622068 | bytes 69660736 | solution.py:134
  188.3 6.1 collective-permute-start.1
  205.9 5.4 collective-permute-start.3
  217.4 14.4 %pad_maximum_fusion.15 = (f32[25,257,130]{2,1,0:T(8,128)}, f32[25,257,130]{2,1,0:T(8,128)}) fusion(f32[25,1,130]{2,1,0:T(1,128)} %collective-permute-done.2, f32[25,256,1]{2,1,0:T(8,128)} %copy.575, f32[25,256,128]{2,1,0:T(8,128)S(1)} %copy.576, f32[25,256,1]{2,1,0:T(8,128)} %copy.577, f32[25,1,130]{2,1,0:T(1,128)} %collective-permute-done.3), kind=kLoop, calls=%fused_computation.9.clone.1 | loop fusion | flops 5011500 | bytes 10036000 | tf_op jit(solution)/shard_map/while/body/eval_jaxpr/concatenate | solution.py:15
  231.8 17.5 %fusion.42 = f32[25,256,128]{2,1,0:T(8,128)} fusion(f32[25,257,130]{2,1,0:T(8,128)} %get-tuple-element.196, f32[25,257,130]{2,1,0:T(8,128)} %get-tuple-element.197, f32[25,256,128]{2,1,0:T(8,128)S(1)} %copy.576, f32[25,256,1]{2,1,0:T(8,128)} %copy.577, f32[25,256,1]{2,1,0:T(8,128)} %copy.575, f32[256,128]{1,0:T(8,128)S(1)} %copy.578, ...), kind=kLoop, calls=%fused_computation.13.clone.1 | loop fusion | flops 15564800 | bytes 26920960 | tf_op jit(solution)/shard_map/while/body/eval_jaxpr/add | solution.py:56
  266.4 5.2 collective-permute-start.3
  277.7 14.4 %pad_maximum_fusion.15 = (f32[25,257,130]{2,1,0:T(8,128)}, f32[25,257,130]{2,1,0:T(8,128)}) fusion(f32[25,1,130]{2,1,0:T(1,128)} %collective-permute-done.2, f32[25,256,1]{2,1,0:T(8,128)} %copy.575, f32[25,256,128]{2,1,0:T(8,128)S(1)} %copy.576, f32[25,256,1]{2,1,0:T(8,128)} %copy.577, f32[25,1,130]{2,1,0:T(1,128)} %collective-permute-done.3), kind=kLoop, calls=%fused_computation.9.clone.1 | loop fusion | flops 5011500 | bytes 10036000 | tf_op jit(solution)/shard_map/while/body/eval_jaxpr/concatenate | solution.py:15
  292.1 17.5 %fusion.42 = f32[25,256,128]{2,1,0:T(8,128)} fusion(f32[25,257,130]{2,1,0:T(8,128)} %get-tuple-element.196, f32[25,257,130]{2,1,0:T(8,128)} %get-tuple-element.197, f32[25,256,128]{2,1,0:T(8,128)S(1)} %copy.576, f32[25,256,1]{2,1,0:T(8,128)} %copy.577, f32[25,256,1]{2,1,0:T(8,128)} %copy.575, f32[256,128]{1,0:T(8,128)S(1)} %copy.578, ...), kind=kLoop, calls=%fused_computation.13.clone.1 | loop fusion | flops 15564800 | bytes 26920960 | tf_op jit(solution)/shard_map/while/body/eval_jaxpr/add | solution.py:56
  326.7 5.2 collective-permute-start.3
  338.0 14.4 %pad_maximum_fusion.15 = (f32[25,257,130]{2,1,0:T(8,128)}, f32[25,257,130]{2,1,0:T(8,128)}) fusion(f32[25,1,130]{2,1,0:T(1,128)} %collective-permute-done.2, f32[25,256,1]{2,1,0:T(8,128)} %copy.575, f32[25,256,128]{2,1,0:T(8,128)S(1)} %copy.576, f32[25,256,1]{2,1,0:T(8,128)} %copy.577, f32[25,1,130]{2,1,0:T(1,128)} %collective-permute-done.3), kind=kLoop, calls=%fused_computation.9.clone.1 | loop fusion | flops 5011500 | bytes 10036000 | tf_op jit(solution)/shard_map/while/body/eval_jaxpr/concatenate | solution.py:15
  352.3 17.5 %fusion.42 = f32[25,256,128]{2,1,0:T(8,128)} fusion(f32[25,257,130]{2,1,0:T(8,128)} %get-tuple-element.196, f32[25,257,130]{2,1,0:T(8,128)} %get-tuple-element.197, f32[25,256,128]{2,1,0:T(8,128)S(1)} %copy.576, f32[25,256,1]{2,1,0:T(8,128)} %copy.577, f32[25,256,1]{2,1,0:T(8,128)} %copy.575, f32[256,128]{1,0:T(8,128)S(1)} %copy.578, ...), kind=kLoop, calls=%fused_computation.13.clone.1 | loop fusion | flops 15564800 | bytes 26920960 | tf_op jit(solution)/shard_map/while/body/eval_jaxpr/add | solution.py:56
  387.9 4.6 collective-permute-start.3
  398.6 14.4 %pad_maximum_fusion.15 = (f32[25,257,130]{2,1,0:T(8,128)}, f32[25,257,130]{2,1,0:T(8,128)}) fusion(f32[25,1,130]{2,1,0:T(1,128)} %collective-permute-done.2, f32[25,256,1]{2,1,0:T(8,128)} %copy.575, f32[25,256,128]{2,1,0:T(8,128)S(1)} %copy.576, f32[25,256,1]{2,1,0:T(8,128)} %copy.577, f32[25,1,130]{2,1,0:T(1,128)} %collective-permute-done.3), kind=kLoop, calls=%fused_computation.9.clone.1 | loop fusion | flops 5011500 | bytes 10036000 | tf_op jit(solution)/shard_map/while/body/eval_jaxpr/concatenate | solution.py:15
  413.0 17.5 %fusion.42 = f32[25,256,128]{2,1,0:T(8,128)} fusion(f32[25,257,130]{2,1,0:T(8,128)} %get-tuple-element.196, f32[25,257,130]{2,1,0:T(8,128)} %get-tuple-element.197, f32[25,256,128]{2,1,0:T(8,128)S(1)} %copy.576, f32[25,256,1]{2,1,0:T(8,128)} %copy.577, f32[25,256,1]{2,1,0:T(8,128)} %copy.575, f32[256,128]{1,0:T(8,128)S(1)} %copy.578, ...), kind=kLoop, calls=%fused_computation.13.clone.1 | loop fusion | flops 15564800 | bytes 26920960 | tf_op jit(solution)/shard_map/while/body/eval_jaxpr/add | solution.py:56
  434.2 5.7 collective-permute-start
  462.1 14.4 %pad_maximum_fusion.15 = (f32[25,257,130]{2,1,0:T(8,128)}, f32[25,257,130]{2,1,0:T(8,128)}) fusion(f32[25,1,130]{2,1,0:T(1,128)} %collective-permute-done.2, f32[25,256,1]{2,1,0:T(8,128)} %copy.575, f32[25,256,128]{2,1,0:T(8,128)S(1)} %copy.576, f32[25,256,1]{2,1,0:T(8,128)} %copy.577, f32[25,1,130]{2,1,0:T(1,128)} %collective-permute-done.3), kind=kLoop, calls=%fused_computation.9.clone.1 | loop fusion | flops 5011500 | bytes 10036000 | tf_op jit(solution)/shard_map/while/body/eval_jaxpr/concatenate | solution.py:15
  476.5 17.5 %fusion.42 = f32[25,256,128]{2,1,0:T(8,128)} fusion(f32[25,257,130]{2,1,0:T(8,128)} %get-tuple-element.196, f32[25,257,130]{2,1,0:T(8,128)} %get-tuple-element.197, f32[25,256,128]{2,1,0:T(8,128)S(1)} %copy.576, f32[25,256,1]{2,1,0:T(8,128)} %copy.577, f32[25,256,1]{2,1,0:T(8,128)} %copy.575, f32[256,128]{1,0:T(8,128)S(1)} %copy.578, ...), kind=kLoop, calls=%fused_computation.13.clone.1 | loop fusion | flops 15564800 | bytes 26920960 | tf_op jit(solution)/shard_map/while/body/eval_jaxpr/add | solution.py:56
  497.7 5.7 collective-permute-start
  514.9 4.6 collective-permute-start.3
  525.6 14.4 %pad_maximum_fusion.15 = (f32[25,257,130]{2,1,0:T(8,128)}, f32[25,257,130]{2,1,0:T(8,128)}) fusion(f32[25,1,130]{2,1,0:T(1,128)} %collective-permute-done.2, f32[25,256,1]{2,1,0:T(8,128)} %copy.575, f32[25,256,128]{2,1,0:T(8,128)S(1)} %copy.576, f32[25,256,1]{2,1,0:T(8,128)} %copy.577, f32[25,1,130]{2,1,0:T(1,128)} %collective-permute-done.3), kind=kLoop, calls=%fused_computation.9.clone.1 | loop fusion | flops 5011500 | bytes 10036000 | tf_op jit(solution)/shard_map/while/body/eval_jaxpr/concatenate | solution.py:15
  540.0 17.5 %fusion.42 = f32[25,256,128]{2,1,0:T(8,128)} fusion(f32[25,257,130]{2,1,0:T(8,128)} %get-tuple-element.196, f32[25,257,130]{2,1,0:T(8,128)} %get-tuple-element.197, f32[25,256,128]{2,1,0:T(8,128)S(1)} %copy.576, f32[25,256,1]{2,1,0:T(8,128)} %copy.577, f32[25,256,1]{2,1,0:T(8,128)} %copy.575, f32[256,128]{1,0:T(8,128)S(1)} %copy.578, ...), kind=kLoop, calls=%fused_computation.13.clone.1 | loop fusion | flops 15564800 | bytes 26920960 | tf_op jit(solution)/shard_map/while/body/eval_jaxpr/add | solution.py:56
  561.2 5.7 collective-permute-start
  589.1 14.4 %pad_maximum_fusion.15 = (f32[25,257,130]{2,1,0:T(8,128)}, f32[25,257,130]{2,1,0:T(8,128)}) fusion(f32[25,1,130]{2,1,0:T(1,128)} %collective-permute-done.2, f32[25,256,1]{2,1,0:T(8,128)} %copy.575, f32[25,256,128]{2,1,0:T(8,128)S(1)} %copy.576, f32[25,256,1]{2,1,0:T(8,128)} %copy.577, f32[25,1,130]{2,1,0:T(1,128)} %collective-permute-done.3), kind=kLoop, calls=%fused_computation.9.clone.1 | loop fusion | flops 5011500 | bytes 10036000 | tf_op jit(solution)/shard_map/while/body/eval_jaxpr/concatenate | solution.py:15
  603.5 17.5 %fusion.42 = f32[25,256,128]{2,1,0:T(8,128)} fusion(f32[25,257,130]{2,1,0:T(8,128)} %get-tuple-element.196, f32[25,257,130]{2,1,0:T(8,128)} %get-tuple-element.197, f32[25,256,128]{2,1,0:T(8,128)S(1)} %copy.576, f32[25,256,1]{2,1,0:T(8,128)} %copy.577, f32[25,256,1]{2,1,0:T(8,128)} %copy.575, f32[256,128]{1,0:T(8,128)S(1)} %copy.578, ...), kind=kLoop, calls=%fused_computation.13.clone.1 | loop fusion | flops 15564800 | bytes 26920960 | tf_op jit(solution)/shard_map/while/body/eval_jaxpr/add | solution.py:56
  624.7 5.7 collective-permute-start
  652.6 14.4 %pad_maximum_fusion.15 = (f32[25,257,130]{2,1,0:T(8,128)}, f32[25,257,130]{2,1,0:T(8,128)}) fusion(f32[25,1,130]{2,1,0:T(1,128)} %collective-permute-done.2, f32[25,256,1]{2,1,0:T(8,128)} %copy.575, f32[25,256,128]{2,1,0:T(8,128)S(1)} %copy.576, f32[25,256,1]{2,1,0:T(8,128)} %copy.577, f32[25,1,130]{2,1,0:T(1,128)} %collective-permute-done.3), kind=kLoop, calls=%fused_computation.9.clone.1 | loop fusion | flops 5011500 | bytes 10036000 | tf_op jit(solution)/shard_map/while/body/eval_jaxpr/concatenate | solution.py:15
  667.0 17.5 %fusion.42 = f32[25,256,128]{2,1,0:T(8,128)} fusion(f32[25,257,130]{2,1,0:T(8,128)} %get-tuple-element.196, f32[25,257,130]{2,1,0:T(8,128)} %get-tuple-element.197, f32[25,256,128]{2,1,0:T(8,128)S(1)} %copy.576, f32[25,256,1]{2,1,0:T(8,128)} %copy.577, f32[25,256,1]{2,1,0:T(8,128)} %copy.575, f32[256,128]{1,0:T(8,128)S(1)} %copy.578, ...), kind=kLoop, calls=%fused_computation.13.clone.1 | loop fusion | flops 15564800 | bytes 26920960 | tf_op jit(solution)/shard_map/while/body/eval_jaxpr/add | solution.py:56
  688.2 5.7 collective-permute-start
  716.2 14.4 %pad_maximum_fusion.15 = (f32[25,257,130]{2,1,0:T(8,128)}, f32[25,257,130]{2,1,0:T(8,128)}) fusion(f32[25,1,130]{2,1,0:T(1,128)} %collective-permute-done.2, f32[25,256,1]{2,1,0:T(8,128)} %copy.575, f32[25,256,128]{2,1,0:T(8,128)S(1)} %copy.576, f32[25,256,1]{2,1,0:T(8,128)} %copy.577, f32[25,1,130]{2,1,0:T(1,128)} %collective-permute-done.3), kind=kLoop, calls=%fused_computation.9.clone.1 | loop fusion | flops 5011500 | bytes 10036000 | tf_op jit(solution)/shard_map/while/body/eval_jaxpr/concatenate | solution.py:15
  730.5 17.5 %fusion.42 = f32[25,256,128]{2,1,0:T(8,128)} fusion(f32[25,257,130]{2,1,0:T(8,128)} %get-tuple-element.196, f32[25,257,130]{2,1,0:T(8,128)} %get-tuple-element.197, f32[25,256,128]{2,1,0:T(8,128)S(1)} %copy.576, f32[25,256,1]{2,1,0:T(8,128)} %copy.577, f32[25,256,1]{2,1,0:T(8,128)} %copy.575, f32[256,128]{1,0:T(8,128)S(1)} %copy.578, ...), kind=kLoop, calls=%fused_computation.13.clone.1 | loop fusion | flops 15564800 | bytes 26920960 | tf_op jit(solution)/shard_map/while/body/eval_jaxpr/add | solution.py:56
  751.7 5.7 collective-permute-start
  779.7 14.4 %pad_maximum_fusion.15 = (f32[25,257,130]{2,1,0:T(8,128)}, f32[25,257,130]{2,1,0:T(8,128)}) fusion(f32[25,1,130]{2,1,0:T(1,128)} %collective-permute-done.2, f32[25,256,1]{2,1,0:T(8,128)} %copy.575, f32[25,256,128]{2,1,0:T(8,128)S(1)} %copy.576, f32[25,256,1]{2,1,0:T(8,128)} %copy.577, f32[25,1,130]{2,1,0:T(1,128)} %collective-permute-done.3), kind=kLoop, calls=%fused_computation.9.clone.1 | loop fusion | flops 5011500 | bytes 10036000 | tf_op jit(solution)/shard_map/while/body/eval_jaxpr/concatenate | solution.py:15
  794.0 17.5 %fusion.42 = f32[25,256,128]{2,1,0:T(8,128)} fusion(f32[25,257,130]{2,1,0:T(8,128)} %get-tuple-element.196, f32[25,257,130]{2,1,0:T(8,128)} %get-tuple-element.197, f32[25,256,128]{2,1,0:T(8,128)S(1)} %copy.576, f32[25,256,1]{2,1,0:T(8,128)} %copy.577, f32[25,256,1]{2,1,0:T(8,128)} %copy.575, f32[256,128]{1,0:T(8,128)S(1)} %copy.578, ...), kind=kLoop, calls=%fused_computation.13.clone.1 | loop fusion | flops 15564800 | bytes 26920960 | tf_op jit(solution)/shard_map/while/body/eval_jaxpr/add | solution.py:56
  821.5 9.0 %copy.564 = f32[25,256,128]{0,2,1:T(8,128)} copy(f32[25,256,128]{2,1,0:T(8,128)S(1)} %mul.199) | data formatting | bytes 6553600 | tf_op jit(solution)/shard_map/mul | solution.py:135
  830.6 8.6 gather_fusion
  839.2 8.6 gather_fusion.1
  847.8 8.6 gather_fusion.2
  856.3 8.8 gather_fusion.3
  867.7 21.8 %all_to_all.37 = f32[128,1,200]{2,1,0:T(1,128)S(1)} all-to-all(f32[128,1,200]{2,1,0:T(1,128)S(1)} %reshape.483), channel_id=1, replica_groups=mesh['lat'=8,'lon'=16] {'lat','lon'}, dimensions={0} | all-to-all | bytes 204800 | tf_op jit(solution)/shard_map/all_to_all | solution.py:144
  (521 shorter events, 308.2 us)
Async XLA Ops:
  5.5 67.9 %collective-permute-start.4 = (f32[4,256,2]{1,2,0:T(2,128)}, f32[4,256,2]{1,2,0:T(2,128)S(1)}, u32[]{:S(2)}, u32[]{:S(2)}) collective-permute-start(f32[4,256,2]{1,2,0:T(2,128)} %get-tuple-element.109), channel_id=1, source_target_pairs={{0,1},{1,2},{2,3},{3,4},{4,5},{5,6},{6,7},{7,8},{8,9},{9,10},{10,1... | collective-permute-start | bytes 24584 | tf_op jit(solution)/shard_map/ppermute | solution.py:17
  8.5 64.9 %collective-permute-start.5 = (f32[4,256,2]{1,2,0:T(2,128)}, f32[4,256,2]{1,2,0:T(2,128)S(1)}, u32[]{:S(2)}, u32[]{:S(2)}) collective-permute-start(f32[4,256,2]{1,2,0:T(2,128)} %get-tuple-element.110), channel_id=1, source_target_pairs={{1,0},{2,1},{3,2},{4,3},{5,4},{6,5},{7,6},{8,7},{9,8},{10,9},{11,1... | collective-permute-start | bytes 24584 | tf_op jit(solution)/shard_map/ppermute | solution.py:19
  10.9 23.2 %all-to-all-start.2 = ((s32[1,16,2]{2,0,1:T(1,128)}), s32[1,16,2]{2,0,1:T(1,128)}, u32[]{:S(2)}, u32[]{:S(2)}) async-start(s32[1,16,2]{2,0,1:T(1,128)} %bitcast.19), calls=%async_computation.2 | async-start | bytes 16384 | tf_op jit(solution)/shard_map/all_to_all | solution.py:86
  34.1 19.0 %all-to-all-start = ((s32[1,128,8]{2,0,1:T(1,128)}), s32[1,128,8]{2,0,1:T(1,128)S(1)}, u32[]{:S(2)}, u32[]{:S(2)}) async-start(s32[1,128,8]{2,0,1:T(1,128)} %bitcast.635), calls=%async_computation | async-start | bytes 131072 | tf_op jit(solution)/shard_map/all_to_all | solution.py:108
  53.2 14.4 %all-to-all-start.1 = ((f32[128,1,232]{2,1,0:T(1,128)}), f32[128,1,232]{2,1,0:T(1,128)S(1)}, u32[]{:S(2)}, u32[]{:S(2)}) async-start(f32[128,1,232]{2,1,0:T(1,128)} %reshape.481), calls=%async_computation.1 | async-start | bytes 262144 | tf_op jit(solution)/shard_map/all_to_all | solution.py:107
  67.6 105.4 %all-to-all-start.3 = ((f32[25,32,8,128]{3,2,0,1:T(8,128)}), f32[25,32,8,128]{3,2,0,1:T(8,128)}, u32[]{:S(2)}, u32[]{:S(2)}) async-start(f32[25,32,8,128]{3,2,0,1:T(8,128)} %copy.555), calls=%async_computation.3 | async-start | bytes 6553600 | tf_op jit(solution)/shard_map/all_to_all | solution.py:85
  73.6 48.7 %collective-permute-start.6 = (f32[4,2,132]{1,2,0:T(8,128)S(1)}, f32[4,2,132]{1,2,0:T(8,128)S(1)}, u32[]{:S(2)}, u32[]{:S(2)}) collective-permute-start(f32[4,2,132]{1,2,0:T(8,128)S(1)} %get-tuple-element.107), channel_id=1, source_target_pairs={{0,16},{16,32},{32,48},{48,64},{64,80},{80,96},{96,112},{1,17},{17... | collective-permute-start | bytes 12680 | tf_op jit(solution)/shard_map/ppermute | solution.py:17
  75.9 46.4 %collective-permute-start.7 = (f32[4,2,132]{1,2,0:T(8,128)S(1)}, f32[4,2,132]{1,2,0:T(8,128)S(1)}, u32[]{:S(2)}, u32[]{:S(2)}) collective-permute-start(f32[4,2,132]{1,2,0:T(8,128)S(1)} %get-tuple-element.108), channel_id=1, source_target_pairs={{16,0},{32,16},{48,32},{64,48},{80,64},{96,80},{112,96},{17,1},{33... | collective-permute-start | bytes 12680 | tf_op jit(solution)/shard_map/ppermute | solution.py:19
  186.7 11.5 %collective-permute-start = (f32[25,256,1]{1,2,0:T(1,128)S(1)}, f32[25,256,1]{1,2,0:T(1,128)S(1)}, u32[]{:S(2)}, u32[]{:S(2)}) collective-permute-start(f32[25,256,1]{1,2,0:T(1,128)S(1)} %get-tuple-element.192), channel_id=1, source_target_pairs={{1,0},{2,1},{3,2},{4,3},{5,4},{6,5},{7,6},{8,7},{9,8},{10,9},{11,1... | collective-permute-start | bytes 76808 | tf_op jit(solution)/shard_map/while/body/eval_jaxpr/ppermute | solution.py:19
  188.3 12.1 %collective-permute-start.1 = (f32[25,256,1]{1,2,0:T(1,128)S(1)}, f32[25,256,1]{1,2,0:T(1,128)S(1)}, u32[]{:S(2)}, u32[]{:S(2)}) collective-permute-start(f32[25,256,1]{1,2,0:T(1,128)S(1)} %get-tuple-element.193), channel_id=1, source_target_pairs={{0,1},{1,2},{2,3},{3,4},{4,5},{5,6},{6,7},{7,8},{8,9},{9,10},{10,1... | collective-permute-start | bytes 76808 | tf_op jit(solution)/shard_map/while/body/eval_jaxpr/ppermute | solution.py:17
  204.6 12.8 %collective-permute-start.2 = (f32[25,1,130]{2,1,0:T(1,128)}, f32[25,1,130]{2,1,0:T(1,128)}, u32[]{:S(2)}, u32[]{:S(2)}) collective-permute-start(f32[25,1,130]{2,1,0:T(1,128)} %get-tuple-element.194), channel_id=1, source_target_pairs={{16,0},{32,16},{48,32},{64,48},{80,64},{96,80},{112,96},{17,1},{33... | collective-permute-start | bytes 39008 | tf_op jit(solution)/shard_map/while/body/eval_jaxpr/ppermute | solution.py:19
  205.9 11.5 %collective-permute-start.3 = (f32[25,1,130]{2,1,0:T(1,128)}, f32[25,1,130]{2,1,0:T(1,128)}, u32[]{:S(2)}, u32[]{:S(2)}) collective-permute-start(f32[25,1,130]{2,1,0:T(1,128)} %get-tuple-element.195), channel_id=1, source_target_pairs={{0,16},{16,32},{32,48},{48,64},{64,80},{80,96},{96,112},{1,17},{17... | collective-permute-start | bytes 39008 | tf_op jit(solution)/shard_map/while/body/eval_jaxpr/ppermute | solution.py:17
  253.0 5.6 collective-permute-start
  254.6 6.3 collective-permute-start.1
  265.1 12.6 %collective-permute-start.2 = (f32[25,1,130]{2,1,0:T(1,128)}, f32[25,1,130]{2,1,0:T(1,128)}, u32[]{:S(2)}, u32[]{:S(2)}) collective-permute-start(f32[25,1,130]{2,1,0:T(1,128)} %get-tuple-element.194), channel_id=1, source_target_pairs={{16,0},{32,16},{48,32},{64,48},{80,64},{96,80},{112,96},{17,1},{33... | collective-permute-start | bytes 39008 | tf_op jit(solution)/shard_map/while/body/eval_jaxpr/ppermute | solution.py:19
  266.4 11.3 %collective-permute-start.3 = (f32[25,1,130]{2,1,0:T(1,128)}, f32[25,1,130]{2,1,0:T(1,128)}, u32[]{:S(2)}, u32[]{:S(2)}) collective-permute-start(f32[25,1,130]{2,1,0:T(1,128)} %get-tuple-element.195), channel_id=1, source_target_pairs={{0,16},{16,32},{32,48},{48,64},{64,80},{80,96},{96,112},{1,17},{17... | collective-permute-start | bytes 39008 | tf_op jit(solution)/shard_map/while/body/eval_jaxpr/ppermute | solution.py:17
  313.3 5.6 collective-permute-start
  314.9 6.3 collective-permute-start.1
  325.4 12.6 %collective-permute-start.2 = (f32[25,1,130]{2,1,0:T(1,128)}, f32[25,1,130]{2,1,0:T(1,128)}, u32[]{:S(2)}, u32[]{:S(2)}) collective-permute-start(f32[25,1,130]{2,1,0:T(1,128)} %get-tuple-element.194), channel_id=1, source_target_pairs={{16,0},{32,16},{48,32},{64,48},{80,64},{96,80},{112,96},{17,1},{33... | collective-permute-start | bytes 39008 | tf_op jit(solution)/shard_map/while/body/eval_jaxpr/ppermute | solution.py:19
  326.7 11.3 %collective-permute-start.3 = (f32[25,1,130]{2,1,0:T(1,128)}, f32[25,1,130]{2,1,0:T(1,128)}, u32[]{:S(2)}, u32[]{:S(2)}) collective-permute-start(f32[25,1,130]{2,1,0:T(1,128)} %get-tuple-element.195), channel_id=1, source_target_pairs={{0,16},{16,32},{32,48},{48,64},{64,80},{80,96},{96,112},{1,17},{17... | collective-permute-start | bytes 39008 | tf_op jit(solution)/shard_map/while/body/eval_jaxpr/ppermute | solution.py:17
  373.5 6.5 collective-permute-start
  376.4 6.0 collective-permute-start.1
  386.6 12.0 %collective-permute-start.2 = (f32[25,1,130]{2,1,0:T(1,128)}, f32[25,1,130]{2,1,0:T(1,128)}, u32[]{:S(2)}, u32[]{:S(2)}) collective-permute-start(f32[25,1,130]{2,1,0:T(1,128)} %get-tuple-element.194), channel_id=1, source_target_pairs={{16,0},{32,16},{48,32},{64,48},{80,64},{96,80},{112,96},{17,1},{33... | collective-permute-start | bytes 39008 | tf_op jit(solution)/shard_map/while/body/eval_jaxpr/ppermute | solution.py:19
  387.9 10.7 %collective-permute-start.3 = (f32[25,1,130]{2,1,0:T(1,128)}, f32[25,1,130]{2,1,0:T(1,128)}, u32[]{:S(2)}, u32[]{:S(2)}) collective-permute-start(f32[25,1,130]{2,1,0:T(1,128)} %get-tuple-element.195), channel_id=1, source_target_pairs={{0,16},{16,32},{32,48},{48,64},{64,80},{80,96},{96,112},{1,17},{17... | collective-permute-start | bytes 39008 | tf_op jit(solution)/shard_map/while/body/eval_jaxpr/ppermute | solution.py:17
  434.2 9.4 %collective-permute-start = (f32[25,256,1]{1,2,0:T(1,128)S(1)}, f32[25,256,1]{1,2,0:T(1,128)S(1)}, u32[]{:S(2)}, u32[]{:S(2)}) collective-permute-start(f32[25,256,1]{1,2,0:T(1,128)S(1)} %get-tuple-element.192), channel_id=1, source_target_pairs={{1,0},{2,1},{3,2},{4,3},{5,4},{6,5},{7,6},{8,7},{9,8},{10,9},{11,1... | collective-permute-start | bytes 76808 | tf_op jit(solution)/shard_map/while/body/eval_jaxpr/ppermute | solution.py:19
  439.9 6.0 collective-permute-start.1
  450.1 12.0 %collective-permute-start.2 = (f32[25,1,130]{2,1,0:T(1,128)}, f32[25,1,130]{2,1,0:T(1,128)}, u32[]{:S(2)}, u32[]{:S(2)}) collective-permute-start(f32[25,1,130]{2,1,0:T(1,128)} %get-tuple-element.194), channel_id=1, source_target_pairs={{16,0},{32,16},{48,32},{64,48},{80,64},{96,80},{112,96},{17,1},{33... | collective-permute-start | bytes 39008 | tf_op jit(solution)/shard_map/while/body/eval_jaxpr/ppermute | solution.py:19
  451.4 10.7 %collective-permute-start.3 = (f32[25,1,130]{2,1,0:T(1,128)}, f32[25,1,130]{2,1,0:T(1,128)}, u32[]{:S(2)}, u32[]{:S(2)}) collective-permute-start(f32[25,1,130]{2,1,0:T(1,128)} %get-tuple-element.195), channel_id=1, source_target_pairs={{0,16},{16,32},{32,48},{48,64},{64,80},{80,96},{96,112},{1,17},{17... | collective-permute-start | bytes 39008 | tf_op jit(solution)/shard_map/while/body/eval_jaxpr/ppermute | solution.py:17
  497.7 9.4 %collective-permute-start = (f32[25,256,1]{1,2,0:T(1,128)S(1)}, f32[25,256,1]{1,2,0:T(1,128)S(1)}, u32[]{:S(2)}, u32[]{:S(2)}) collective-permute-start(f32[25,256,1]{1,2,0:T(1,128)S(1)} %get-tuple-element.192), channel_id=1, source_target_pairs={{1,0},{2,1},{3,2},{4,3},{5,4},{6,5},{7,6},{8,7},{9,8},{10,9},{11,1... | collective-permute-start | bytes 76808 | tf_op jit(solution)/shard_map/while/body/eval_jaxpr/ppermute | solution.py:19
  503.4 6.0 collective-permute-start.1
  513.6 12.0 %collective-permute-start.2 = (f32[25,1,130]{2,1,0:T(1,128)}, f32[25,1,130]{2,1,0:T(1,128)}, u32[]{:S(2)}, u32[]{:S(2)}) collective-permute-start(f32[25,1,130]{2,1,0:T(1,128)} %get-tuple-element.194), channel_id=1, source_target_pairs={{16,0},{32,16},{48,32},{64,48},{80,64},{96,80},{112,96},{17,1},{33... | collective-permute-start | bytes 39008 | tf_op jit(solution)/shard_map/while/body/eval_jaxpr/ppermute | solution.py:19
  514.9 10.7 %collective-permute-start.3 = (f32[25,1,130]{2,1,0:T(1,128)}, f32[25,1,130]{2,1,0:T(1,128)}, u32[]{:S(2)}, u32[]{:S(2)}) collective-permute-start(f32[25,1,130]{2,1,0:T(1,128)} %get-tuple-element.195), channel_id=1, source_target_pairs={{0,16},{16,32},{32,48},{48,64},{64,80},{80,96},{96,112},{1,17},{17... | collective-permute-start | bytes 39008 | tf_op jit(solution)/shard_map/while/body/eval_jaxpr/ppermute | solution.py:17
  561.2 9.4 %collective-permute-start = (f32[25,256,1]{1,2,0:T(1,128)S(1)}, f32[25,256,1]{1,2,0:T(1,128)S(1)}, u32[]{:S(2)}, u32[]{:S(2)}) collective-permute-start(f32[25,256,1]{1,2,0:T(1,128)S(1)} %get-tuple-element.192), channel_id=1, source_target_pairs={{1,0},{2,1},{3,2},{4,3},{5,4},{6,5},{7,6},{8,7},{9,8},{10,9},{11,1... | collective-permute-start | bytes 76808 | tf_op jit(solution)/shard_map/while/body/eval_jaxpr/ppermute | solution.py:19
  566.9 6.0 collective-permute-start.1
  577.1 12.0 %collective-permute-start.2 = (f32[25,1,130]{2,1,0:T(1,128)}, f32[25,1,130]{2,1,0:T(1,128)}, u32[]{:S(2)}, u32[]{:S(2)}) collective-permute-start(f32[25,1,130]{2,1,0:T(1,128)} %get-tuple-element.194), channel_id=1, source_target_pairs={{16,0},{32,16},{48,32},{64,48},{80,64},{96,80},{112,96},{17,1},{33... | collective-permute-start | bytes 39008 | tf_op jit(solution)/shard_map/while/body/eval_jaxpr/ppermute | solution.py:19
  578.4 10.7 %collective-permute-start.3 = (f32[25,1,130]{2,1,0:T(1,128)}, f32[25,1,130]{2,1,0:T(1,128)}, u32[]{:S(2)}, u32[]{:S(2)}) collective-permute-start(f32[25,1,130]{2,1,0:T(1,128)} %get-tuple-element.195), channel_id=1, source_target_pairs={{0,16},{16,32},{32,48},{48,64},{64,80},{80,96},{96,112},{1,17},{17... | collective-permute-start | bytes 39008 | tf_op jit(solution)/shard_map/while/body/eval_jaxpr/ppermute | solution.py:17
  624.7 9.4 %collective-permute-start = (f32[25,256,1]{1,2,0:T(1,128)S(1)}, f32[25,256,1]{1,2,0:T(1,128)S(1)}, u32[]{:S(2)}, u32[]{:S(2)}) collective-permute-start(f32[25,256,1]{1,2,0:T(1,128)S(1)} %get-tuple-element.192), channel_id=1, source_target_pairs={{1,0},{2,1},{3,2},{4,3},{5,4},{6,5},{7,6},{8,7},{9,8},{10,9},{11,1... | collective-permute-start | bytes 76808 | tf_op jit(solution)/shard_map/while/body/eval_jaxpr/ppermute | solution.py:19
  630.4 6.0 collective-permute-start.1
  640.6 12.0 %collective-permute-start.2 = (f32[25,1,130]{2,1,0:T(1,128)}, f32[25,1,130]{2,1,0:T(1,128)}, u32[]{:S(2)}, u32[]{:S(2)}) collective-permute-start(f32[25,1,130]{2,1,0:T(1,128)} %get-tuple-element.194), channel_id=1, source_target_pairs={{16,0},{32,16},{48,32},{64,48},{80,64},{96,80},{112,96},{17,1},{33... | collective-permute-start | bytes 39008 | tf_op jit(solution)/shard_map/while/body/eval_jaxpr/ppermute | solution.py:19
  641.9 10.7 %collective-permute-start.3 = (f32[25,1,130]{2,1,0:T(1,128)}, f32[25,1,130]{2,1,0:T(1,128)}, u32[]{:S(2)}, u32[]{:S(2)}) collective-permute-start(f32[25,1,130]{2,1,0:T(1,128)} %get-tuple-element.195), channel_id=1, source_target_pairs={{0,16},{16,32},{32,48},{48,64},{64,80},{80,96},{96,112},{1,17},{17... | collective-permute-start | bytes 39008 | tf_op jit(solution)/shard_map/while/body/eval_jaxpr/ppermute | solution.py:17
  688.2 9.4 %collective-permute-start = (f32[25,256,1]{1,2,0:T(1,128)S(1)}, f32[25,256,1]{1,2,0:T(1,128)S(1)}, u32[]{:S(2)}, u32[]{:S(2)}) collective-permute-start(f32[25,256,1]{1,2,0:T(1,128)S(1)} %get-tuple-element.192), channel_id=1, source_target_pairs={{1,0},{2,1},{3,2},{4,3},{5,4},{6,5},{7,6},{8,7},{9,8},{10,9},{11,1... | collective-permute-start | bytes 76808 | tf_op jit(solution)/shard_map/while/body/eval_jaxpr/ppermute | solution.py:19
  693.9 6.0 collective-permute-start.1
  704.1 12.0 %collective-permute-start.2 = (f32[25,1,130]{2,1,0:T(1,128)}, f32[25,1,130]{2,1,0:T(1,128)}, u32[]{:S(2)}, u32[]{:S(2)}) collective-permute-start(f32[25,1,130]{2,1,0:T(1,128)} %get-tuple-element.194), channel_id=1, source_target_pairs={{16,0},{32,16},{48,32},{64,48},{80,64},{96,80},{112,96},{17,1},{33... | collective-permute-start | bytes 39008 | tf_op jit(solution)/shard_map/while/body/eval_jaxpr/ppermute | solution.py:19
  705.4 10.7 %collective-permute-start.3 = (f32[25,1,130]{2,1,0:T(1,128)}, f32[25,1,130]{2,1,0:T(1,128)}, u32[]{:S(2)}, u32[]{:S(2)}) collective-permute-start(f32[25,1,130]{2,1,0:T(1,128)} %get-tuple-element.195), channel_id=1, source_target_pairs={{0,16},{16,32},{32,48},{48,64},{64,80},{80,96},{96,112},{1,17},{17... | collective-permute-start | bytes 39008 | tf_op jit(solution)/shard_map/while/body/eval_jaxpr/ppermute | solution.py:17
  751.7 9.4 %collective-permute-start = (f32[25,256,1]{1,2,0:T(1,128)S(1)}, f32[25,256,1]{1,2,0:T(1,128)S(1)}, u32[]{:S(2)}, u32[]{:S(2)}) collective-permute-start(f32[25,256,1]{1,2,0:T(1,128)S(1)} %get-tuple-element.192), channel_id=1, source_target_pairs={{1,0},{2,1},{3,2},{4,3},{5,4},{6,5},{7,6},{8,7},{9,8},{10,9},{11,1... | collective-permute-start | bytes 76808 | tf_op jit(solution)/shard_map/while/body/eval_jaxpr/ppermute | solution.py:19
  757.4 6.0 collective-permute-start.1
  767.6 12.0 %collective-permute-start.2 = (f32[25,1,130]{2,1,0:T(1,128)}, f32[25,1,130]{2,1,0:T(1,128)}, u32[]{:S(2)}, u32[]{:S(2)}) collective-permute-start(f32[25,1,130]{2,1,0:T(1,128)} %get-tuple-element.194), channel_id=1, source_target_pairs={{16,0},{32,16},{48,32},{64,48},{80,64},{96,80},{112,96},{17,1},{33... | collective-permute-start | bytes 39008 | tf_op jit(solution)/shard_map/while/body/eval_jaxpr/ppermute | solution.py:19
  768.9 10.7 %collective-permute-start.3 = (f32[25,1,130]{2,1,0:T(1,128)}, f32[25,1,130]{2,1,0:T(1,128)}, u32[]{:S(2)}, u32[]{:S(2)}) collective-permute-start(f32[25,1,130]{2,1,0:T(1,128)} %get-tuple-element.195), channel_id=1, source_target_pairs={{0,16},{16,32},{32,48},{48,64},{64,80},{80,96},{96,112},{1,17},{17... | collective-permute-start | bytes 39008 | tf_op jit(solution)/shard_map/while/body/eval_jaxpr/ppermute | solution.py:17
  (57 other events, 743.3 us)
